TPU v7x, 32 devices: a whole 2x2x4 slice. The times are simulated.
32 devices in a mesh: lon: 8 (over y, x, core), lat: 4 (over z).
Axes of the slice: x: 2, y: 2, z: 4, core: 2. Of those that a mesh axis runs over, the one named last changes fastest.
Arguments:
- initial_kelvin_map: float32 [512, 256, 128], P('lon', 'lat'), may hold values from -6 to 6
- thermal_diffusivity_map: float32 [512, 256, 128], P('lon', 'lat'), may hold values from 0.1 to 1
- interior_power_source: float32 [512, 256, 128], P('lon', 'lat'), may hold values from -6 to 6
- earlier_east_west_basis: float32 [512, 32], P('lon'), may hold values from -0.25 to 0.25
- earlier_north_south_basis: float32 [256, 32], P('lat'), may hold values from -0.375 to 0.375
- earlier_depthwise_basis: float32 [128, 32], replicated, may hold values from -0.5 to 0.5
Outputs:
- final_kelvin_map: float32 [512, 256, 128], P('lon', 'lat')
- error: float32 [512, 256, 128], P('lon', 'lat')
- new_lon: float32 [512, 32], P('lon')
- new_lat: float32 [256, 32], P('lat')
- new_rad: float32 [128, 32], replicated
- core: float32 [32, 32, 32], replicated
All inputs are finite; a program needn't handle non-finite values.
Results may differ from a plain program's by a relative error of at most 0.02.
Values sent between devices are 32-bit elements; how exact they have to be, the bound alone decides.
A program may use at most 64 MiB of HBM per device.

v0:
```python
import jax
import jax.numpy as jnp
from jax import lax
from jax.sharding import PartitionSpec as P

SHELL_LAYERS = 128
R = 32
STEPS = 4


highest = lax.Precision.HIGHEST
time_step = 0.15


def extended(x, sides, width, wrap):
    for axis, dim in sides:
        count, length = (lax.axis_size(axis), x.shape[dim])
        up = [(i, (i + 1) % count) for i in range(count if wrap else count - 1)]
        down = [(j, i) for i, j in up]
        last = lax.slice_in_dim(x, length - width, length, axis=dim)
        initial = lax.slice_in_dim(x, 0, width, axis=dim)
        before = lax.ppermute(last, axis, up)
        after = lax.ppermute(initial, axis, down)
        x = jnp.concatenate([before, x, after], axis=dim)
    return x


def harmonic(cond_a, cond_b):
    summed = cond_a + cond_b
    return 2.0 * cond_a * cond_b / jnp.where(summed > 0.0, summed, 1.0)


def advance(padded, cond_pad, interior_power_source):
    centre = padded[1:-1, 1:-1]
    kcentre = cond_pad[1:-1, 1:-1]
    change = interior_power_source
    pairs = (
        (padded[2:, 1:-1], cond_pad[2:, 1:-1]),
        (padded[:-2, 1:-1], cond_pad[:-2, 1:-1]),
        (padded[1:-1, 2:], cond_pad[1:-1, 2:]),
        (padded[1:-1, :-2], cond_pad[1:-1, :-2]),
    )
    for near_t, near_k in pairs:
        change = change + harmonic(kcentre, near_k) * (near_t - centre)
    radial_t = jnp.pad(centre, ((0, 0), (0, 0), (1, 1)))
    radial_k = jnp.pad(kcentre, ((0, 0), (0, 0), (1, 1)))
    change = change + harmonic(kcentre, radial_k[:, :, 2:]) * (radial_t[:, :, 2:] - centre)
    change = change + harmonic(kcentre, radial_k[:, :, :-2]) * (radial_t[:, :, :-2] - centre)
    return centre + time_step * change


def orthonormal(block, gram):
    factor_l = jnp.linalg.cholesky(gram)
    return lax.linalg.triangular_solve(
        factor_l, block, left_side=False, lower=True, transpose_a=True
    )


def local(
    initial_kelvin_map,
    thermal_diffusivity_map,
    interior_power_source,
    earlier_east_west_basis,
    earlier_north_south_basis,
    earlier_depthwise_basis,
):
    east_west_entries = initial_kelvin_map.shape[0]
    north_south_entries = initial_kelvin_map.shape[1]
    cond_lon = extended(thermal_diffusivity_map, (("lon", 0),), 1, True)
    cond_pad = extended(cond_lon, (("lat", 1),), 1, False)
    final_kelvin_map = initial_kelvin_map
    for step_index in range(STEPS):
        temp_lon = extended(final_kelvin_map, (("lon", 0),), 1, True)
        padded = extended(temp_lon, (("lat", 1),), 1, False)
        final_kelvin_map = advance(padded, cond_pad, interior_power_source)
    rad_proj = jnp.dot(
        final_kelvin_map.reshape(east_west_entries * north_south_entries, SHELL_LAYERS),
        earlier_depthwise_basis,
        precision=highest,
    ).reshape(east_west_entries, north_south_entries, R)
    modes = jnp.einsum(
        "ijb,ja->iab", rad_proj, earlier_north_south_basis, precision=highest
    ).reshape(east_west_entries, R * R)
    modes = lax.psum(modes, "lat")
    proj = lax.psum(jnp.dot(modes.T, earlier_east_west_basis, precision=highest), "lon")
    block = jnp.dot(modes, proj, precision=highest)
    gram = lax.psum(jnp.dot(block.T, block, precision=highest), "lon")
    new_lon = orthonormal(block, gram)
    modes = jnp.einsum("ijb,ia->jab", rad_proj, new_lon, precision=highest).reshape(
        north_south_entries, R * R
    )
    modes = lax.psum(modes, "lon")
    proj = lax.psum(jnp.dot(modes.T, earlier_north_south_basis, precision=highest), "lat")
    block = jnp.dot(modes, proj, precision=highest)
    gram = lax.psum(jnp.dot(block.T, block, precision=highest), "lat")
    new_lat = orthonormal(block, gram)
    lon_proj = jnp.dot(
        new_lon.T,
        final_kelvin_map.reshape(east_west_entries, north_south_entries * SHELL_LAYERS),
        precision=highest,
    ).reshape(R, north_south_entries, SHELL_LAYERS)
    local_modes = jnp.einsum("ajr,jb->rab", lon_proj, new_lat, precision=highest)
    part = lax.psum_scatter(local_modes, "lon", scatter_dimension=1, tiled=True)
    part = lax.psum(part, "lat")
    proj = jnp.einsum("rab,rc->abc", part, earlier_depthwise_basis, precision=highest)
    block = lax.psum(jnp.einsum("rab,abc->rc", part, proj, precision=highest), "lon")
    gram = jnp.dot(block.T, block, precision=highest)
    new_rad = orthonormal(block, gram)
    piece = jnp.einsum("rab,rc->abc", part, new_rad, precision=highest)
    core = lax.all_gather(piece, "lon", axis=0, tiled=True)
    first = jnp.einsum("abc,rc->abr", core, new_rad, precision=highest)
    second = jnp.einsum("abr,jb->ajr", first, new_lat, precision=highest)
    recon = jnp.dot(
        new_lon, second.reshape(R, north_south_entries * SHELL_LAYERS), precision=highest
    ).reshape(east_west_entries, north_south_entries, SHELL_LAYERS)
    return (final_kelvin_map, final_kelvin_map - recon, new_lon, new_lat, new_rad, core)


def solution(mesh):
    in_specs = (
        P("lon", "lat", None),
        P("lon", "lat", None),
        P("lon", "lat", None),
        P("lon", None),
        P("lat", None),
        P(),
    )
    out_specs = (
        P("lon", "lat", None),
        P("lon", "lat", None),
        P("lon", None),
        P("lat", None),
        P(),
        P(),
    )
    return jax.shard_map(local, mesh=mesh, in_specs=in_specs, out_specs=out_specs, check_vma=False)
```

profile of v0, /device:TPU:0, one launch (start us, length us, event | category | flops | bytes accessed | tf_op | source)
XLA Modules:
  0.0 487.8 jit_solution(4317118117336477257)
XLA Ops:
  8.5 2.9 collective-permute-start
  12.9 3.0 copy.96
  18.6 4.6 collective-permute-start.6
  24.5 4.6 collective-permute-start.7
  30.7 8.6 %fusion.5 = (f32[64,64,128]{2,0,1:T(8,128)S(1)}, f32[64,64,128]{2,0,1:T(8,128)S(1)}, f32[64,64,128]{2,0,1:T(8,128)S(1)}) fusion(f32[64,64,128]{2,0,1:T(8,128)S(1)} %copy.122, f32[66,1,128]{2,0,1:T(8,128)S(1)} %collective-permute-done.7, f32[1,64,128]{2,0,1:T(1,128)S(1)} %collective-permute-done.1, f32[1,64,128]{2,0,1:T(1,128)S(1)} %collective-permute-done.3, ...), kind=kLoop, calls=%fused_computation.21 | loop fusion | flops 35127296 | bytes 12849152 | tf_op jit(solution)/shard_map/add | solution.py:49
  45.0 4.9 collective-permute-start.11
  51.5 7.7 %fusion.13 = f32[64,64,128]{2,0,1:T(8,128)S(1)} fusion(f32[64,64,128]{2,0,1:T(8,128)S(1)} %get-tuple-element.26, f32[64,64,128]{2,0,1:T(8,128)S(1)} %get-tuple-element.28, f32[64,64,128]{2,0,1:T(8,128)S(1)} %get-tuple-element.27, f32[66,1,128]{2,0,1:T(8,128)S(1)} %collective-permute-done.11, f32[1,64,128]{2,0,1:T(1,128)S(1)} %collective-permute-done.8, ...), kind=kLoop, calls=%fused_computation.29 | loop fusion | flops 29884416 | bytes 12849152 | tf_op jit(solution)/shard_map/add | solution.py:49
  64.8 4.9 %collective-permute-start.15 = (f32[66,1,128]{2,0,1:T(8,128)S(1)}, f32[66,1,128]{2,0,1:T(8,128)S(1)}, u32[]{:S(2)}, u32[]{:S(2)}) collective-permute-start(f32[66,1,128]{2,0,1:T(8,128)S(1)} %get-tuple-element.32), channel_id=1, source_target_pairs={{0,1},{1,2},{2,3},{4,5},{5,6},{6,7},{8,9},{9,10},{10,11},{12,13},{... | collective-permute-start | bytes 101384 | tf_op jit(solution)/shard_map/ppermute | solution.py:22
  71.4 7.7 %fusion.21 = f32[64,64,128]{2,0,1:T(8,128)S(1)} fusion(f32[64,64,128]{2,0,1:T(8,128)S(1)} %fusion.13, f32[64,64,128]{2,0,1:T(8,128)S(1)} %get-tuple-element.28, f32[64,64,128]{2,0,1:T(8,128)S(1)} %get-tuple-element.27, f32[66,1,128]{2,0,1:T(8,128)S(1)} %collective-permute-done.15, f32[1,64,128]{2,0,1:T(1,128)S(1)} %collective-permute-done.12, ...), kind=kLoop, calls=%fused_computation.37 | loop fusion | flops 29884416 | bytes 12849152 | tf_op jit(solution)/shard_map/add | solution.py:49
  85.0 4.9 collective-permute-start.19
  91.3 7.7 %fusion.29 = f32[64,64,128]{2,0,1:T(8,128)S(1)} fusion(f32[64,64,128]{2,0,1:T(8,128)S(1)} %fusion.21, f32[64,64,128]{2,0,1:T(8,128)S(1)} %get-tuple-element.28, f32[64,64,128]{2,0,1:T(8,128)S(1)} %get-tuple-element.27, f32[66,1,128]{2,0,1:T(8,128)S(1)} %collective-permute-done.19, f32[1,64,128]{2,0,1:T(1,128)S(1)} %collective-permute-done.16, ...), kind=kLoop, calls=%fused_computation.45 | loop fusion | flops 29884416 | bytes 12849152 | tf_op jit(solution)/shard_map/add | solution.py:49
  99.0 6.7 %fusion.125 = f32[64,64,32]{0,2,1:T(8,128)} fusion(f32[64,64,128]{2,0,1:T(8,128)S(1)} %fusion.29, f32[128,32]{0,1:T(8,128)S(1)} %copy-done), kind=kOutput, calls=%fused_computation.209 | convolution fusion | flops 201326592 | bytes 2637824 | tf_op jit(solution)/shard_map/dot_general | solution.py:76
  107.5 2.9 convolution_bitcast_fusion.2
  111.6 41.1 %all-reduce.11.cloned.1.call-done = f32[64,1024]{0,1:T(8,128)} async-done(((f32[64,1024]{0,1:T(8,128)}), f32[64,1024]{0,1:T(8,128)}) %all-reduce.11.cloned.1.call-update) | async-done | bytes 262160 | tf_op jit(solution)/shard_map/psum | solution.py:84
  155.2 54.5 %all-reduce.13.cloned.1.call-done = f32[1024,32]{0,1:T(8,128)} async-done(((f32[1024,32]{0,1:T(8,128)}), f32[1024,32]{0,1:T(8,128)}) %all-reduce.13.cloned.1.call-update) | async-done | bytes 131088 | tf_op jit(solution)/shard_map/psum | solution.py:85
  211.3 22.3 %psum.58 = f32[32,32]{0,1:T(8,128)S(1)} all-reduce(f32[32,32]{0,1:T(8,128)S(1)} %fusion.136), channel_id=1, replica_groups=mesh['lon'=8,'lat'=4] {'lon'}, use_global_device_ids=true, to_apply=%region_2.3 | all-reduce | flops 1024 | bytes 8192 | tf_op jit(solution)/shard_map/psum | solution.py:87
  242.4 54.3 %all-reduce.15.cloned.1.call-done = f32[64,1024]{0,1:T(8,128)} async-done(((f32[64,1024]{0,1:T(8,128)}), f32[64,1024]{0,1:T(8,128)}) %all-reduce.15.cloned.1.call-update) | async-done | bytes 262160 | tf_op jit(solution)/shard_map/psum | solution.py:92
  300.5 33.0 %all-reduce.17.cloned.1.call-done = f32[1024,32]{0,1:T(8,128)} async-done(((f32[1024,32]{0,1:T(8,128)}), f32[1024,32]{0,1:T(8,128)}) %all-reduce.17.cloned.1.call-update) | async-done | bytes 131088 | tf_op jit(solution)/shard_map/psum | solution.py:93
  335.1 17.5 %psum.61 = f32[32,32]{0,1:T(8,128)S(1)} all-reduce(f32[32,32]{0,1:T(8,128)S(1)} %fusion.139), channel_id=1, replica_groups=mesh['lon'=8,'lat'=4] {'lat'}, use_global_device_ids=true, to_apply=%region_7.10 | all-reduce | flops 1024 | bytes 8192 | tf_op jit(solution)/shard_map/psum | solution.py:95
  352.7 2.9 cholesky.70
  361.8 32.3 %reduce-scatter.2.cloned.1.call-done = f32[128,4,32]{0,2,1:T(8,128)} async-done(((f32[128,32,32]{0,2,1:T(8,128)}), f32[128,4,32]{0,2,1:T(8,128)}) %reduce-scatter.2.cloned.1.call-update) | async-done | bytes 65552 | tf_op jit(solution)/shard_map/reduce_scatter | solution.py:103
  396.6 33.9 %all-reduce.19.cloned.1.call-done = f32[128,4,32]{0,2,1:T(8,128)} async-done(((f32[128,4,32]{0,2,1:T(8,128)}), f32[128,4,32]{0,2,1:T(8,128)}) %all-reduce.19.cloned.1.call-update) | async-done | bytes 65552 | tf_op jit(solution)/shard_map/psum | solution.py:104
  432.9 22.3 %psum.63 = f32[128,32]{0,1:T(8,128)S(1)} all-reduce(f32[128,32]{0,1:T(8,128)S(1)} %convolution_bitcast_fusion.3), channel_id=1, replica_groups=mesh['lon'=8,'lat'=4] {'lon'}, use_global_device_ids=true, to_apply=%region_10.13 | all-reduce | flops 4096 | bytes 32768 | tf_op jit(solution)/shard_map/psum | solution.py:106
  463.5 10.1 %all_gather.3 = f32[32,32,32]{2,1,0:T(8,128)S(1)} all-gather(f32[4,32,32]{2,1,0:T(8,128)S(1)} %fusion.105), channel_id=1, replica_groups=mesh['lon'=8,'lat'=4] {'lon'}, dimensions={0}, use_global_device_ids=true | all-gather | bytes 147456 | tf_op jit(solution)/shard_map/all_gather | solution.py:110
  (118 shorter events, 77.7 us)
Async XLA Ops:
  7.2 145.6 %all-reduce.11.cloned.1.call-start = ((), (), s32[]{:S(2)}) async-start(), calls=%async_computation.1 | async-start | bytes 1048576 | tf_op jit(solution)/shard_map/psum | solution.py:84
  8.0 9.1 %collective-permute-start.2 = (f32[1,64,128]{2,0,1:T(1,128)S(1)}, f32[1,64,128]{2,0,1:T(1,128)S(1)}, u32[]{:S(2)}, u32[]{:S(2)}) collective-permute-start(f32[1,64,128]{2,0,1:T(1,128)S(1)} %bitcast.135), channel_id=1, source_target_pairs={{0,4},{4,8},{8,12},{12,16},{16,20},{20,24},{24,28},{28,0},{1,5},{5... | collective-permute-start | bytes 98312 | tf_op jit(solution)/shard_map/ppermute | solution.py:22
  8.5 8.6 %collective-permute-start = (f32[1,64,128]{2,0,1:T(1,128)S(1)}, f32[1,64,128]{2,0,1:T(1,128)S(1)}, u32[]{:S(2)}, u32[]{:S(2)}) collective-permute-start(f32[1,64,128]{2,0,1:T(1,128)S(1)} %bitcast.134), channel_id=1, source_target_pairs={{4,0},{8,4},{12,8},{16,12},{20,16},{24,20},{28,24},{0,28},{5,1},{9... | collective-permute-start | bytes 98312 | tf_op jit(solution)/shard_map/ppermute | solution.py:23
  12.2 11.0 %collective-permute-start.1 = (f32[1,64,128]{2,0,1:T(1,128)S(1)}, f32[1,64,128]{2,0,1:T(1,128)S(1)}, u32[]{:S(2)}, u32[]{:S(2)}) collective-permute-start(f32[1,64,128]{2,0,1:T(1,128)S(1)} %bitcast.133), channel_id=1, source_target_pairs={{4,0},{8,4},{12,8},{16,12},{20,16},{24,20},{28,24},{0,28},{5,1},{9... | collective-permute-start | bytes 98312 | tf_op jit(solution)/shard_map/ppermute | solution.py:23
  12.9 10.3 %collective-permute-start.3 = (f32[1,64,128]{2,0,1:T(1,128)S(1)}, f32[1,64,128]{2,0,1:T(1,128)S(1)}, u32[]{:S(2)}, u32[]{:S(2)}) collective-permute-start(f32[1,64,128]{2,0,1:T(1,128)S(1)} %bitcast.132), channel_id=1, source_target_pairs={{0,4},{4,8},{8,12},{12,16},{16,20},{20,24},{24,28},{28,0},{1,5},{5... | collective-permute-start | bytes 98312 | tf_op jit(solution)/shard_map/ppermute | solution.py:22
  17.1 12.0 %collective-permute-start.4 = (f32[66,1,128]{2,0,1:T(8,128)S(1)}, f32[66,1,128]{2,0,1:T(8,128)S(1)}, u32[]{:S(2)}, u32[]{:S(2)}) collective-permute-start(f32[66,1,128]{2,0,1:T(8,128)S(1)} %get-tuple-element.35), channel_id=1, source_target_pairs={{1,0},{2,1},{3,2},{5,4},{6,5},{7,6},{9,8},{10,9},{11,10},{13,12},{... | collective-permute-start | bytes 101384 | tf_op jit(solution)/shard_map/ppermute | solution.py:23
  18.6 10.5 %collective-permute-start.6 = (f32[66,1,128]{2,0,1:T(8,128)S(1)}, f32[66,1,128]{2,0,1:T(8,128)S(1)}, u32[]{:S(2)}, u32[]{:S(2)}) collective-permute-start(f32[66,1,128]{2,0,1:T(8,128)S(1)} %get-tuple-element.36), channel_id=1, source_target_pairs={{0,1},{1,2},{2,3},{4,5},{5,6},{6,7},{8,9},{9,10},{10,11},{12,13},{... | collective-permute-start | bytes 101384 | tf_op jit(solution)/shard_map/ppermute | solution.py:22
  23.2 5.9 %collective-permute-start.5 = (f32[66,1,128]{2,0,1:T(8,128)S(1)}, f32[66,1,128]{2,0,1:T(8,128)S(1)}, u32[]{:S(2)}, u32[]{:S(2)}) collective-permute-start(f32[66,1,128]{2,0,1:T(8,128)S(1)} %get-tuple-element.37), channel_id=1, source_target_pairs={{1,0},{2,1},{3,2},{5,4},{6,5},{7,6},{9,8},{10,9},{11,10},{13,12},{... | collective-permute-start | bytes 101384 | tf_op jit(solution)/shard_map/ppermute | solution.py:23
  24.5 6.2 %collective-permute-start.7 = (f32[66,1,128]{2,0,1:T(8,128)S(1)}, f32[66,1,128]{2,0,1:T(8,128)S(1)}, u32[]{:S(2)}, u32[]{:S(2)}) collective-permute-start(f32[66,1,128]{2,0,1:T(8,128)S(1)} %get-tuple-element.38), channel_id=1, source_target_pairs={{0,1},{1,2},{2,3},{4,5},{5,6},{6,7},{8,9},{9,10},{10,11},{12,13},{... | collective-permute-start | bytes 101384 | tf_op jit(solution)/shard_map/ppermute | solution.py:22
  39.4 4.3 collective-permute-start.9
  43.7 6.5 %collective-permute-start.10 = (f32[66,1,128]{2,0,1:T(8,128)S(1)}, f32[66,1,128]{2,0,1:T(8,128)S(1)}, u32[]{:S(2)}, u32[]{:S(2)}) collective-permute-start(f32[66,1,128]{2,0,1:T(8,128)S(1)} %get-tuple-element.33), channel_id=1, source_target_pairs={{1,0},{2,1},{3,2},{5,4},{6,5},{7,6},{9,8},{10,9},{11,10},{13,12},{... | collective-permute-start | bytes 101384 | tf_op jit(solution)/shard_map/ppermute | solution.py:23
  45.0 6.5 %collective-permute-start.11 = (f32[66,1,128]{2,0,1:T(8,128)S(1)}, f32[66,1,128]{2,0,1:T(8,128)S(1)}, u32[]{:S(2)}, u32[]{:S(2)}) collective-permute-start(f32[66,1,128]{2,0,1:T(8,128)S(1)} %get-tuple-element.34), channel_id=1, source_target_pairs={{0,1},{1,2},{2,3},{4,5},{5,6},{6,7},{8,9},{9,10},{10,11},{12,13},{... | collective-permute-start | bytes 101384 | tf_op jit(solution)/shard_map/ppermute | solution.py:22
  59.2 4.3 collective-permute-start.13
  63.5 6.3 %collective-permute-start.14 = (f32[66,1,128]{2,0,1:T(8,128)S(1)}, f32[66,1,128]{2,0,1:T(8,128)S(1)}, u32[]{:S(2)}, u32[]{:S(2)}) collective-permute-start(f32[66,1,128]{2,0,1:T(8,128)S(1)} %get-tuple-element.31), channel_id=1, source_target_pairs={{1,0},{2,1},{3,2},{5,4},{6,5},{7,6},{9,8},{10,9},{11,10},{13,12},{... | collective-permute-start | bytes 101384 | tf_op jit(solution)/shard_map/ppermute | solution.py:23
  64.8 6.6 %collective-permute-start.15 = (f32[66,1,128]{2,0,1:T(8,128)S(1)}, f32[66,1,128]{2,0,1:T(8,128)S(1)}, u32[]{:S(2)}, u32[]{:S(2)}) collective-permute-start(f32[66,1,128]{2,0,1:T(8,128)S(1)} %get-tuple-element.32), channel_id=1, source_target_pairs={{0,1},{1,2},{2,3},{4,5},{5,6},{6,7},{8,9},{9,10},{10,11},{12,13},{... | collective-permute-start | bytes 101384 | tf_op jit(solution)/shard_map/ppermute | solution.py:22
  79.2 4.5 collective-permute-start.17
  79.2 4.4 collective-permute-start.16
  83.7 6.2 %collective-permute-start.18 = (f32[66,1,128]{2,0,1:T(8,128)S(1)}, f32[66,1,128]{2,0,1:T(8,128)S(1)}, u32[]{:S(2)}, u32[]{:S(2)}) collective-permute-start(f32[66,1,128]{2,0,1:T(8,128)S(1)} %get-tuple-element.29), channel_id=1, source_target_pairs={{1,0},{2,1},{3,2},{5,4},{6,5},{7,6},{9,8},{10,9},{11,10},{13,12},{... | collective-permute-start | bytes 101384 | tf_op jit(solution)/shard_map/ppermute | solution.py:23
  85.0 6.3 %collective-permute-start.19 = (f32[66,1,128]{2,0,1:T(8,128)S(1)}, f32[66,1,128]{2,0,1:T(8,128)S(1)}, u32[]{:S(2)}, u32[]{:S(2)}) collective-permute-start(f32[66,1,128]{2,0,1:T(8,128)S(1)} %get-tuple-element.30), channel_id=1, source_target_pairs={{0,1},{1,2},{2,3},{4,5},{5,6},{6,7},{8,9},{9,10},{10,11},{12,13},{... | collective-permute-start | bytes 101384 | tf_op jit(solution)/shard_map/ppermute | solution.py:22
  111.6 98.1 %all-reduce.13.cloned.1.call-start = ((), (), s32[]{:S(2)}) async-start(), calls=%async_computation.2 | async-start | bytes 262144 | tf_op jit(solution)/shard_map/psum | solution.py:85
  155.1 141.7 %all-reduce.15.cloned.1.call-start = ((), (), s32[]{:S(2)}) async-start(), calls=%async_computation.3 | async-start | bytes 1048576 | tf_op jit(solution)/shard_map/psum | solution.py:92
  242.4 91.1 %all-reduce.17.cloned.1.call-start = ((), (), s32[]{:S(2)}) async-start(), calls=%async_computation.4 | async-start | bytes 262144 | tf_op jit(solution)/shard_map/psum | solution.py:93
  299.1 94.9 %reduce-scatter.2.cloned.1.call-start = ((), (), s32[]{:S(2)}) async-start(), calls=%async_computation.5 | async-start | bytes 589824 | tf_op jit(solution)/shard_map/reduce_scatter | solution.py:103
  361.7 68.9 %all-reduce.19.cloned.1.call-start = ((), (), s32[]{:S(2)}) async-start(), calls=%async_computation.6 | async-start | bytes 131072 | tf_op jit(solution)/shard_map/psum | solution.py:104
  (10 other events, 534.8 us)
Sparse Core Ops, SparseCore 0:
  111.7 40.9 all-reduce.10
  156.3 53.2 all-reduce.12
  242.5 54.2 all-reduce.14
  299.5 33.9 all-reduce.16
  361.8 32.2 reduce-scatter.1
  396.2 34.2 all-reduce.18
where the time goes:
time: 489 us; the launch traced here: 488 us
  waiting for transfers between devices  260 us (53%)
  blocking collectives  72.2 us (15%)
  other arithmetic  51.9 us (11%)
  starting transfers between devices  43 us (9%)
  matrix products  29.5 us (6%)
  local copies, waits for them, and re-layouts  16 us (3%)
  between operations  14.6 us (3%)
    psum x1, waiting for transfers between devices, local(): lax.psum(jnp.dot(modes.T, earlier_east_west_basis, precision=highest), 'l...  54.5 us
    psum x1, waiting for transfers between devices, local(): modes = lax.psum(modes, 'lon')  54.3 us
    psum x1, waiting for transfers between devices, local(): modes = lax.psum(modes, 'lat')  41.1 us
    psum x1, waiting for transfers between devices, local(): part = lax.psum(part, 'lat')  33.9 us
    psum x1, waiting for transfers between devices, local(): lax.psum(jnp.dot(modes.T, earlier_north_south_basis, precision=highest),...  33 us
    reduce_scatter x1, waiting for transfers between devices, local(): part = lax.psum_scatter(local_modes, 'lon', scatter_dimension=1, tiled=True)  32.3 us
    add x4, other arithmetic, advance(): return centre + time_step * change  31.7 us
    ppermute x10, starting transfers between devices, extended(): before = lax.ppermute(last, axis, up)  24.5 us
  transfers between devices with their start and end apart: 26, of which 14 were waited for; matrix products, arithmetic and copies ran while one was open for 2% of the time, Pallas kernels for 0%

commit v1 on v0

v1 whole, which is shorter than its diff:
```python
import functools

import jax
import jax.numpy as jnp
from jax import lax
from jax.experimental import pallas as pl
from jax.experimental.pallas import tpu as pltpu
from jax.sharding import PartitionSpec as P

STEPS = 4
time_step = 0.15
F32 = jnp.float32
BF16 = jnp.bfloat16
NN = (((1,), (0,)), ((), ()))
NT = (((1,), (1,)), ((), ()))
TN = (((0,), (0,)), ((), ()))


def split(x):
    hi = x.astype(BF16)
    return hi, (x - hi.astype(F32)).astype(BF16)


def dot3(a, b, dims=NN):
    ah, al = a
    bh, bl = b
    d = functools.partial(lax.dot_general, dimension_numbers=dims, preferred_element_type=F32)
    return d(ah, bh) + d(ah, bl) + d(al, bh)


def mm(a, b, dims=NN):
    return dot3(split(a), split(b), dims)


def mmh(a, b, dims=NN):
    return lax.dot_general(
        a, b, dims, precision=lax.Precision.HIGHEST, preferred_element_type=F32
    )


def chol_inverse(gram):
    n = gram.shape[0]
    row = lax.broadcasted_iota(jnp.int32, (n, n), 0)
    col = lax.broadcasted_iota(jnp.int32, (n, n), 1)
    eye = jnp.where(row == col, 1.0, 0.0).astype(F32)
    m = jnp.concatenate([gram, eye], axis=1)
    rows = lax.broadcasted_iota(jnp.int32, (n, 1), 0)
    for k in range(n - 1):
        top = m[k : k + 1, :]
        factor = jnp.where(rows > k, m[:, k : k + 1] / m[k : k + 1, k : k + 1], 0.0)
        m = m - factor * top
    diag = jnp.sum(jnp.where(row == col, m[:, :n], 0.0), axis=1, keepdims=True)
    return m[:, n:] / jnp.sqrt(diag)


def block_diag(x, count):
    n = x.shape[0]
    wide = jnp.concatenate([x] * count, axis=1)
    full = jnp.concatenate([wide] * count, axis=0)
    row = lax.broadcasted_iota(jnp.int32, full.shape, 0) // n
    col = lax.broadcasted_iota(jnp.int32, full.shape, 1) // n
    return jnp.where(row == col, full, 0.0)


class Comm:
    def __init__(self, nl, nz, send_sem, recv_sem):
        self.nl, self.nz = nl, nz
        self.lon = lax.axis_index("lon")
        self.lat = lax.axis_index("lat")
        self.send_sem, self.recv_sem = send_sem, recv_sem
        self.phase = 0
        self.sent = []

    def start(self, axis, source, target):
        count = self.nl if axis == "lon" else self.nz
        me = self.lon if axis == "lon" else self.lat
        ph = self.phase
        self.phase += 1
        waits = []
        for d in range(1, count):
            peer = lax.rem(me + d, count)
            owner = lax.rem(me + count - d, count)
            copy = pltpu.make_async_remote_copy(
                src_ref=source(peer),
                dst_ref=target(me),
                send_sem=self.send_sem.at[ph, d],
                recv_sem=self.recv_sem.at[ph, d],
                device_id={axis: peer},
                device_id_type=pl.DeviceIdType.MESH,
            )
            copy.start()
            self.sent.append(copy)
            waits.append(
                pltpu.make_async_remote_copy(
                    src_ref=target(owner),
                    dst_ref=target(owner),
                    send_sem=self.send_sem.at[ph, d],
                    recv_sem=self.recv_sem.at[ph, d],
                    device_id={axis: peer},
                    device_id_type=pl.DeviceIdType.MESH,
                )
            )
        return waits

    def gather(self, axis, slots):
        me = self.lon if axis == "lon" else self.lat
        return self.start(axis, lambda peer: slots.at[me], lambda owner: slots.at[owner])

    def wait(self, waits):
        for w in waits:
            w.wait_recv()

    def finish(self):
        for c in self.sent:
            c.wait_send()


def total(slots):
    out = slots[0]
    for k in range(1, slots.shape[0]):
        out = out + slots[k]
    return out


def all_reduce(comm, buf, rs, zs, ag, during=None):
    rows = rs.shape[1]
    piece = lambda ref, p: ref.at[pl.ds(pl.multiple_of(p * rows, rows), rows)]
    first = comm.start("lon", lambda peer: piece(buf, peer), lambda owner: rs.at[owner])
    rs[comm.lon] = piece(buf, comm.lon)[...]
    if during is not None:
        during[0]()
    comm.wait(first)
    zs[comm.lat] = total(rs)
    second = comm.gather("lat", zs)
    if during is not None:
        during[1]()
    comm.wait(second)
    piece(ag, comm.lon)[...] = total(zs)
    third = comm.start("lon", lambda peer: piece(ag, comm.lon), lambda owner: piece(ag, owner))
    if during is not None:
        during[2]()
    comm.wait(third)


def sweep_kernel(nl, nz, t_ref, u_ref, v_ref, w_ref,
                 err_ref, lon_ref, lat_ref, rad_ref, core_ref,
                 z1, x3, y3, f_ref, y1, y2, small,
                 b1s, b2s, b3l, b3z, g1s, g2s, bufs, rss, zss, ags,
                 send_sem, recv_sem):
    comm = Comm(nl, nz, send_sem, recv_sem)
    ni, nj, nr = t_ref.shape
    r = u_ref.shape[1]
    group = 128 // r
    blocks = r // group

    barrier = pltpu.get_barrier_semaphore()
    for d in range(1, nl):
        pl.semaphore_signal(barrier, inc=1, device_id={"lon": lax.rem(comm.lon + d, nl)},
                            device_id_type=pl.DeviceIdType.MESH)
    for d in range(1, nz):
        pl.semaphore_signal(barrier, inc=1, device_id={"lat": lax.rem(comm.lat + d, nz)},
                            device_id_type=pl.DeviceIdType.MESH)

    wt = w_ref[...].T
    wts = split(wt)
    ut = u_ref[...].T
    vt = v_ref[...].T

    @pl.loop(0, ni // 8)
    def _(step):
        for k in range(8):
            i = step * 8 + k
            z1[:, i, :] = dot3(wts, split(t_ref[i]), NT)

    lane = lambda n: lax.broadcasted_iota(jnp.int32, (n, 128), 1) // r
    v4 = split(jnp.concatenate([v_ref[...]] * group, axis=1))
    uts = split(ut)
    for m in range(blocks):
        out = jnp.zeros((ni, 128), F32)
        for g in range(group):
            out = jnp.where(lane(ni) == g, dot3(split(z1[m * group + g]), v4), out)
        y1[m] = out
        bufs[0, pl.ds(m * r, r), :] = dot3(uts, split(out))

    pl.semaphore_wait(barrier, nl + nz - 2)

    all_reduce(comm, bufs.at[0], rss.at[0], zss.at[0], ags.at[0])

    acc = jnp.zeros((r, ni), F32)
    for m in range(blocks):
        acc = acc + mm(ags[0, pl.ds(m * r, r), :], y1[m], NT)
    b1s[comm.lat] = acc
    w = comm.gather("lat", b1s)
    comm.wait(w)
    b1t = total(b1s)
    g1s[comm.lon] = mmh(b1t, b1t, NT)
    g1w = comm.gather("lon", g1s)
    b1x = split(jnp.concatenate([b1t] * group, axis=0).T)
    vts = split(vt)
    for m in range(blocks):
        out = jnp.zeros((nj, 128), F32)
        for g in range(group):
            out = jnp.where(lane(nj) == g, dot3(split(z1[m * group + g]), b1x, TN), out)
        y2[m] = out
        bufs[1, pl.ds(m * r, r), :] = dot3(vts, split(out))

    def chol1():
        comm.wait(g1w)
        small[0] = chol_inverse(total(g1s))

    nothing = lambda: None
    all_reduce(comm, bufs.at[1], rss.at[1], zss.at[1], ags.at[1], (nothing, chol1, nothing))

    l1 = small[0]
    bd1 = split(block_diag(mmh(l1, l1, TN), group))
    acc = jnp.zeros((r, nj), F32)
    for m in range(blocks):
        acc = acc + mm(dot3(split(ags[1, pl.ds(m * r, r), :]), bd1), y2[m], NT)
    b2s[comm.lon] = acc
    w = comm.gather("lon", b2s)
    lont = mmh(l1, b1t)
    lon_ref[...] = lont.T
    comm.wait(w)
    b2t = total(b2s)
    g2s[comm.lat] = mmh(b2t, b2t, NT)
    g2w = comm.gather("lat", g2s)
    b2h = split(b2t)

    @pl.loop(0, ni // 8)
    def _(step):
        for k in range(8):
            i = step * 8 + k
            x3[i] = dot3(b2h, split(t_ref[i]))

    lonh = split(lont)
    for b in range(r):
        y3[:, b, :] = dot3(lonh, split(x3[:, b, :]))

    per = 128 // r

    def y3block(m):
        return split(y3[pl.ds(m * per, per)].reshape(128, nr))

    for m in range(blocks):
        bufs[2, pl.ds(m * r, r), :] = dot3(wts, y3block(m), NT)

    def chol2():
        comm.wait(g2w)
        small[1] = chol_inverse(total(g2s))

    all_reduce(comm, bufs.at[2], rss.at[2], zss.at[2], ags.at[2], (chol2, nothing, nothing))

    l2 = small[1]
    bd2 = split(block_diag(mmh(l2, l2, TN), group))
    acc = jnp.zeros((r, nr), F32)
    for m in range(blocks):
        acc = acc + dot3(split(dot3(split(ags[2, pl.ds(m * r, r), :]), bd2)), y3block(m))
    b3l[comm.lon] = acc
    w = comm.gather("lon", b3l)
    latt = mmh(l2, b2t)
    lat_ref[...] = latt.T
    comm.wait(w)
    b3z[comm.lat] = total(b3l)
    w = comm.gather("lat", b3z)
    comm.wait(w)
    b3t = total(b3z)
    l3 = chol_inverse(mmh(b3t, b3t, NT))
    radt = mmh(l3, b3t)
    rad_ref[...] = radt.T
    radh = split(radt)
    for m in range(blocks):
        bufs[3, pl.ds(m * r, r), :] = dot3(radh, y3block(m), NT)
    all_reduce(comm, bufs.at[3], rss.at[3], zss.at[3], ags.at[3])

    bdl = split(block_diag(l2.T, group))
    for m in range(blocks):
        core = dot3(split(ags[3, pl.ds(m * r, r), :]), bdl)
        core_ref[pl.ds(m * 128, 128), :] = core.T
        f_ref[pl.ds(m * per, per)] = dot3(split(core), radh, TN).reshape(per, r, nr)
    lonb = split(lon_ref[...])
    latb = split(lat_ref[...])
    for b in range(r):
        x3[:, b, :] = dot3(lonb, split(f_ref[:, b, :]))

    @pl.loop(0, ni // 8)
    def _(step):
        for k in range(8):
            i = step * 8 + k
            err_ref[i] = t_ref[i] - dot3(latb, split(x3[i]))

    comm.finish()


def sweep(t, u, v, w):
    nl, nz = lax.axis_size("lon"), lax.axis_size("lat")
    ni, nj, nr = t.shape
    r = u.shape[1]
    rows = r * r * r // 128
    piece = rows // nl
    blocks = r * r // 128
    most = max(nl, nz)
    vm = pl.BlockSpec(memory_space=pltpu.VMEM)
    sds = lambda *s: jax.ShapeDtypeStruct(s, F32)
    V = lambda *s: pltpu.VMEM(s, F32)
    phases = 18
    err, lon, lat, rad, core = pl.pallas_call(
        functools.partial(sweep_kernel, nl, nz),
        out_shape=(sds(ni, nj, nr), sds(ni, r), sds(nj, r), sds(nr, r), sds(r * r, r)),
        in_specs=[vm] * 4,
        out_specs=(vm,) * 5,
        scratch_shapes=[
            V(r, ni, nj), V(ni, r, nr), V(r, r, nr), V(r, r, nr),
            V(blocks, ni, 128), V(blocks, nj, 128), V(2, r, r),
            V(nz, r, ni), V(nl, r, nj), V(nl, r, nr), V(nz, r, nr),
            V(nl, r, r), V(nz, r, r),
            V(4, rows, 128), V(4, nl, piece, 128), V(4, nz, piece, 128), V(4, rows, 128),
            pltpu.SemaphoreType.DMA((phases, most)),
            pltpu.SemaphoreType.DMA((phases, most)),
        ],
        compiler_params=pltpu.CompilerParams(
            collective_id=1, has_side_effects=True, vmem_limit_bytes=40 * 1024 * 1024
        ),
    )(t, u, v, w)
    return err, lon, lat, rad, core.reshape(r, r, r)


def extended(x, sides, width, wrap):
    for axis, dim in sides:
        count, length = (lax.axis_size(axis), x.shape[dim])
        up = [(i, (i + 1) % count) for i in range(count if wrap else count - 1)]
        down = [(j, i) for i, j in up]
        last = lax.slice_in_dim(x, length - width, length, axis=dim)
        initial = lax.slice_in_dim(x, 0, width, axis=dim)
        before = lax.ppermute(last, axis, up)
        after = lax.ppermute(initial, axis, down)
        x = jnp.concatenate([before, x, after], axis=dim)
    return x


def harmonic(cond_a, cond_b):
    summed = cond_a + cond_b
    return 2.0 * cond_a * cond_b / jnp.where(summed > 0.0, summed, 1.0)


def advance(padded, cond_pad, interior_power_source):
    centre = padded[1:-1, 1:-1]
    kcentre = cond_pad[1:-1, 1:-1]
    change = interior_power_source
    pairs = (
        (padded[2:, 1:-1], cond_pad[2:, 1:-1]),
        (padded[:-2, 1:-1], cond_pad[:-2, 1:-1]),
        (padded[1:-1, 2:], cond_pad[1:-1, 2:]),
        (padded[1:-1, :-2], cond_pad[1:-1, :-2]),
    )
    for near_t, near_k in pairs:
        change = change + harmonic(kcentre, near_k) * (near_t - centre)
    radial_t = jnp.pad(centre, ((0, 0), (0, 0), (1, 1)))
    radial_k = jnp.pad(kcentre, ((0, 0), (0, 0), (1, 1)))
    change = change + harmonic(kcentre, radial_k[:, :, 2:]) * (radial_t[:, :, 2:] - centre)
    change = change + harmonic(kcentre, radial_k[:, :, :-2]) * (radial_t[:, :, :-2] - centre)
    return centre + time_step * change


def local(temp, cond, source, lon_basis, lat_basis, rad_basis):
    cond_lon = extended(cond, (("lon", 0),), 1, True)
    cond_pad = extended(cond_lon, (("lat", 1),), 1, False)
    for _ in range(STEPS):
        temp_lon = extended(temp, (("lon", 0),), 1, True)
        padded = extended(temp_lon, (("lat", 1),), 1, False)
        temp = advance(padded, cond_pad, source)
    err, lon, lat, rad, core = sweep(temp, lon_basis, lat_basis, rad_basis)
    return temp, err, lon, lat, rad, core


def solution(mesh):
    grid = P("lon", "lat", None)
    in_specs = (grid, grid, grid, P("lon", None), P("lat", None), P())
    out_specs = (grid, grid, P("lon", None), P("lat", None), P(), P())
    return jax.shard_map(local, mesh=mesh, in_specs=in_specs, out_specs=out_specs, check_vma=False)
```

time: 489 us -> 190 us (0.39)
  waiting for transfers between devices: 260 us -> 17.2 us
  Pallas kernels: 0 us -> 86.4 us
  blocking collectives: 72.2 us -> 0 us
  matrix products: 29.5 us -> 0 us
  other arithmetic: 51.9 us -> 34.7 us
  between operations: 14.6 us -> 1.08 us
    psum x5 -> x0, waiting for transfers between devices: 217 us -> none  [the longest x1 54.5 us: local(): lax.psum(jnp.dot(modes.T, earlier_east_west_basis, precision=highest), 'l...]
    pallas_call x0 -> x1, Pallas kernels: none -> 86.4 us  [sweep(): pl.pallas_call(functools.partial(sweep_kernel, nl, nz), out_shape=(sds(ni...]
    psum x3 -> x0, blocking collectives: 62.1 us -> none  [the longest x1 22.3 us: local(): gram = lax.psum(jnp.dot(block.T, block, precision=highest), 'lon')]
    reduce_scatter x1 -> x0, waiting for transfers between devices: 32.3 us -> none  [local(): part = lax.psum_scatter(local_modes, 'lon', scatter_dimension=1, tiled=True)]
    dot_general x18 -> x0, matrix products: 28.8 us -> none  [the longest x1 6.75 us: local(): jnp.dot(final_kelvin_map.reshape(east_west_entries * north_south_entries,...]
    another operation x15 -> x0, other arithmetic: 20.1 us -> none  [the longest x9 10.8 us: orthonormal(): factor_l = jnp.linalg.cholesky(gram)]
    all_gather x1 -> x0, blocking collectives: 10.1 us -> none  [local(): core = lax.all_gather(piece, 'lon', axis=0, tiled=True)]
    ppermute x10, starting transfers between devices: 18.1 us -> 12.5 us  [extended(): after = lax.ppermute(initial, axis, down)]
  transfers between devices with their start and end apart: 26 -> 20, of which waited for: 14 -> 10; matrix products, arithmetic and copies ran while one was open for 2% -> 2% of each run, Pallas kernels for 0% -> 0%
where the time goes in v1:
time: 190 us
  Pallas kernels  86.4 us (45%)
  starting transfers between devices  38.6 us (20%)
  other arithmetic  34.7 us (18%)
  waiting for transfers between devices  17.2 us (9%)
  local copies, waits for them, and re-layouts  11.6 us (6%)
    pallas_call x1, Pallas kernels, sweep(): pl.pallas_call(functools.partial(sweep_kernel, nl, nz), out_shape=(sds(ni...  86.4 us
    add x4, other arithmetic, advance(): return centre + time_step * change  34.5 us
    ppermute x10, starting transfers between devices, extended(): before = lax.ppermute(last, axis, up)  26.1 us
    ppermute x10, waiting for transfers between devices, extended(): before = lax.ppermute(last, axis, up)  13.9 us
    ppermute x10, starting transfers between devices, extended(): after = lax.ppermute(initial, axis, down)  12.5 us
    unnamed x38, local copies, waits for them, and re-layouts  9.88 us
  transfers between devices with their start and end apart: 20, of which 10 were waited for; matrix products, arithmetic and copies ran while one was open for 2% of the time, Pallas kernels for 0%

profile of v1, /device:TPU:0, one launch (start us, length us, event | category | flops | bytes accessed | tf_op | source)
XLA Modules:
  0.0 189.5 jit_solution(3651296113426449974)
XLA Ops:
  1.9 2.9 %collective-permute-start = (f32[1,64,128]{2,1,0:T(8,128)S(1)}, f32[1,64,128]{2,1,0:T(8,128)S(1)}, u32[]{:S(2)}, u32[]{:S(2)}) collective-permute-start(f32[1,64,128]{2,1,0:T(8,128)S(1)} %get-tuple-element.43), channel_id=1, source_target_pairs={{4,0},{8,4},{12,8},{16,12},{20,16},{24,20},{28,24},{0,28},{5,1},{9... | collective-permute-start | bytes 98312 | tf_op jit(solution)/shard_map/ppermute | solution.py:335
  5.6 2.6 %collective-permute-start.1 = (f32[1,64,128]{2,1,0:T(8,128)S(1)}, f32[1,64,128]{2,1,0:T(8,128)S(1)}, u32[]{:S(2)}, u32[]{:S(2)}) collective-permute-start(f32[1,64,128]{2,1,0:T(8,128)S(1)} %get-tuple-element.45), channel_id=1, source_target_pairs={{4,0},{8,4},{12,8},{16,12},{20,16},{24,20},{28,24},{0,28},{5,1},{9... | collective-permute-start | bytes 98312 | tf_op jit(solution)/shard_map/ppermute | solution.py:335
  8.3 2.0 %constant_dynamic-update-slice_fusion.1 = f32[66,64,128]{2,1,0:T(8,128)S(1)} fusion(f32[66,64,128]{2,1,0:T(8,128)S(1)} %constant_dynamic-update-slice_fusion.2, f32[64,64,128]{2,1,0:T(8,128)} %param.7), kind=kLoop, calls=%fused_computation.148 | loop fusion | bytes 4194304
  10.3 1.3 collective-permute-start.4
  11.6 4.8 %collective-permute-start.6 = (f32[66,1,128]{2,1,0:T(1,128)S(1)}, f32[66,1,128]{2,1,0:T(1,128)S(1)}, u32[]{:S(2)}, u32[]{:S(2)}) collective-permute-start(f32[66,1,128]{2,1,0:T(1,128)S(1)} %get-tuple-element.33), channel_id=1, source_target_pairs={{0,1},{1,2},{2,3},{4,5},{5,6},{6,7},{8,9},{9,10},{10,11},{12,13},{... | collective-permute-start | bytes 101384 | tf_op jit(solution)/shard_map/ppermute | solution.py:334
  16.8 1.6 collective-permute-start.5
  18.4 4.6 %collective-permute-start.7 = (f32[66,1,128]{2,1,0:T(1,128)S(1)}, f32[66,1,128]{2,1,0:T(1,128)S(1)}, u32[]{:S(2)}, u32[]{:S(2)}) collective-permute-start(f32[66,1,128]{2,1,0:T(1,128)S(1)} %get-tuple-element.36), channel_id=1, source_target_pairs={{0,1},{1,2},{2,3},{4,5},{5,6},{6,7},{8,9},{9,10},{10,11},{12,13},{... | collective-permute-start | bytes 101384 | tf_op jit(solution)/shard_map/ppermute | solution.py:334
  23.0 1.6 collective-permute-done.7
  24.6 7.8 %fusion.5 = (f32[64,64,128]{2,1,0:T(8,128)S(1)}, f32[64,64,128]{2,1,0:T(8,128)S(1)}, f32[64,64,128]{2,1,0:T(8,128)S(1)}, f32[64,64,128]{2,1,0:T(8,128)S(1)}, f32[64,64,128]{2,1,0:T(8,128)S(1)}) fusion(f32[64,64,128]{2,1,0:T(8,128)S(1)} %copy-done.9, f32[66,64,128]{2,1,0:T(8,128)S(1)} %constant_dynamic-update-slice_fusion.3, ...), kind=kLoop, calls=%fused_computation.21 | loop fusion | flops 30932992 | bytes 21368832 | tf_op jit(solution)/shard_map/add | solution.py:361
  34.1 2.7 %collective-permute-done.9 = f32[1,64,128]{2,1,0:T(8,128)S(1)} collective-permute-done((f32[1,64,128]{2,1,0:T(8,128)S(1)}, f32[1,64,128]{2,1,0:T(8,128)S(1)}, u32[]{:S(2)}, u32[]{:S(2)}) %collective-permute-start.9) | collective-permute-done | bytes 32800 | tf_op jit(solution)/shard_map/ppermute | solution.py:334
  38.1 4.9 %collective-permute-start.11 = (f32[66,1,128]{2,1,0:T(1,128)S(1)}, f32[66,1,128]{2,1,0:T(1,128)S(1)}, u32[]{:S(2)}, u32[]{:S(2)}) collective-permute-start(f32[66,1,128]{2,1,0:T(1,128)S(1)} %get-tuple-element.32), channel_id=1, source_target_pairs={{0,1},{1,2},{2,3},{4,5},{5,6},{6,7},{8,9},{9,10},{10,11},{12,13},{... | collective-permute-start | bytes 101384 | tf_op jit(solution)/shard_map/ppermute | solution.py:334
  43.0 1.6 collective-permute-done.11
  44.6 5.5 %fusion.13 = f32[64,64,128]{2,1,0:T(8,128)S(1)} fusion(f32[64,64,128]{2,1,0:T(8,128)S(1)} %get-tuple-element.22, f32[64,64,128]{2,1,0:T(8,128)S(1)} %get-tuple-element.26, f32[64,64,128]{2,1,0:T(8,128)S(1)} %get-tuple-element.25, f32[64,64,128]{2,1,0:T(8,128)S(1)} %get-tuple-element.24, f32[66,1,128]{2,1,0:T(1,128)S(1)} %collective-permute-done.11, ...), kind=kLoop, calls=%fused_computation.29 | loop fusion | flops 21495808 | bytes 16975872 | tf_op jit(solution)/shard_map/add | solution.py:361
  51.8 2.7 %collective-permute-done.13 = f32[1,64,128]{2,1,0:T(8,128)S(1)} collective-permute-done((f32[1,64,128]{2,1,0:T(8,128)S(1)}, f32[1,64,128]{2,1,0:T(8,128)S(1)}, u32[]{:S(2)}, u32[]{:S(2)}) %collective-permute-start.13) | collective-permute-done | bytes 32800 | tf_op jit(solution)/shard_map/ppermute | solution.py:334
  54.5 1.3 collective-permute-start.14
  55.8 4.9 %collective-permute-start.15 = (f32[66,1,128]{2,1,0:T(1,128)S(1)}, f32[66,1,128]{2,1,0:T(1,128)S(1)}, u32[]{:S(2)}, u32[]{:S(2)}) collective-permute-start(f32[66,1,128]{2,1,0:T(1,128)S(1)} %get-tuple-element.30), channel_id=1, source_target_pairs={{0,1},{1,2},{2,3},{4,5},{5,6},{6,7},{8,9},{9,10},{10,11},{12,13},{... | collective-permute-start | bytes 101384 | tf_op jit(solution)/shard_map/ppermute | solution.py:334
  60.7 1.6 collective-permute-done.15
  62.3 5.5 %fusion.21 = f32[64,64,128]{2,1,0:T(8,128)S(1)} fusion(f32[64,64,128]{2,1,0:T(8,128)S(1)} %fusion.13, f32[64,64,128]{2,1,0:T(8,128)S(1)} %get-tuple-element.26, f32[64,64,128]{2,1,0:T(8,128)S(1)} %get-tuple-element.25, f32[64,64,128]{2,1,0:T(8,128)S(1)} %get-tuple-element.24, f32[66,1,128]{2,1,0:T(1,128)S(1)} %collective-permute-done.15, ...), kind=kLoop, calls=%fused_computation.37 | loop fusion | flops 21495808 | bytes 16975872 | tf_op jit(solution)/shard_map/add | solution.py:361
  69.5 2.7 %collective-permute-done.17 = f32[1,64,128]{2,1,0:T(8,128)S(1)} collective-permute-done((f32[1,64,128]{2,1,0:T(8,128)S(1)}, f32[1,64,128]{2,1,0:T(8,128)S(1)}, u32[]{:S(2)}, u32[]{:S(2)}) %collective-permute-start.17) | collective-permute-done | bytes 32800 | tf_op jit(solution)/shard_map/ppermute | solution.py:334
  73.6 5.0 %collective-permute-start.19 = (f32[66,1,128]{2,1,0:T(1,128)S(1)}, f32[66,1,128]{2,1,0:T(1,128)S(1)}, u32[]{:S(2)}, u32[]{:S(2)}) collective-permute-start(f32[66,1,128]{2,1,0:T(1,128)S(1)} %get-tuple-element.28), channel_id=1, source_target_pairs={{0,1},{1,2},{2,3},{4,5},{5,6},{6,7},{8,9},{9,10},{10,11},{12,13},{... | collective-permute-start | bytes 101384 | tf_op jit(solution)/shard_map/ppermute | solution.py:334
  80.1 15.7 %fusion.29.t_ref = f32[64,64,128]{2,1,0:T(8,128)S(1)} fusion(f32[64,64,128]{2,1,0:T(8,128)} %copy-done.8, f32[64,64,128]{2,1,0:T(8,128)} %copy-done.7, f32[64,64,128]{2,1,0:T(8,128)} %copy-done.6, f32[64,64,128]{2,1,0:T(8,128)} %copy-done.5, f32[66,1,128]{2,1,0:T(1,128)S(1)} %collective-permute-done.19, f32[1,64,128]{2,1,0:T(8,128)S(1)} %collective-permute-done.16, ...), kind=kLoop, calls=%fused_computation.45 | loop fusion | flops 21495808 | bytes 16975872 | tf_op jit(solution)/shard_map/add | solution.py:361
  95.8 86.4 %shard_map.109 = (f32[64,64,128]{2,1,0:T(8,128)S(1)}, f32[64,32]{1,0:T(8,128)S(1)}, f32[64,32]{1,0:T(8,128)S(1)}, f32[128,32]{1,0:T(8,128)S(1)}, f32[1024,32]{1,0:T(8,128)S(1)}) custom-call(f32[64,64,128]{2,1,0:T(8,128)S(1)} %fusion.29.t_ref, f32[64,32]{1,0:T(8,128)S(1)} %copy.12.u_ref, f32[64,32]{1,0:T(8,128)S(1)} %copy.13.v_ref, f32[128,32]{1,0:T(8,128)S(1)} %copy.14.w_ref), custom_call_target="tpu_custom_call" | custom-call | tf_op jit(solution)/shard_map/pallas_call | solution.py:306
  182.2 1.3 copy-done.1
  185.6 3.2 %copy.24 = f32[64,64,128]{2,1,0:T(8,128)} copy(f32[64,64,128]{2,1,0:T(8,128)} %copy-done.1) | data formatting | bytes 4194304
  (71 shorter events, 14.4 us)
Async XLA Ops:
  1.4 6.8 %collective-permute-start.2 = (f32[1,64,128]{2,1,0:T(8,128)S(1)}, f32[1,64,128]{2,1,0:T(8,128)S(1)}, u32[]{:S(2)}, u32[]{:S(2)}) collective-permute-start(f32[1,64,128]{2,1,0:T(8,128)S(1)} %get-tuple-element.44), channel_id=1, source_target_pairs={{0,4},{4,8},{8,12},{12,16},{16,20},{20,24},{24,28},{28,0},{1,5},{5... | collective-permute-start | bytes 98312 | tf_op jit(solution)/shard_map/ppermute | solution.py:334
  1.9 8.3 %collective-permute-start = (f32[1,64,128]{2,1,0:T(8,128)S(1)}, f32[1,64,128]{2,1,0:T(8,128)S(1)}, u32[]{:S(2)}, u32[]{:S(2)}) collective-permute-start(f32[1,64,128]{2,1,0:T(8,128)S(1)} %get-tuple-element.43), channel_id=1, source_target_pairs={{4,0},{8,4},{12,8},{16,12},{20,16},{24,20},{28,24},{0,28},{5,1},{9... | collective-permute-start | bytes 98312 | tf_op jit(solution)/shard_map/ppermute | solution.py:335
  5.6 10.8 %collective-permute-start.3 = (f32[1,64,128]{2,1,0:T(8,128)S(1)}, f32[1,64,128]{2,1,0:T(8,128)S(1)}, u32[]{:S(2)}, u32[]{:S(2)}) collective-permute-start(f32[1,64,128]{2,1,0:T(8,128)S(1)} %get-tuple-element.46), channel_id=1, source_target_pairs={{0,4},{4,8},{8,12},{12,16},{16,20},{20,24},{24,28},{28,0},{1,5},{5... | collective-permute-start | bytes 98312 | tf_op jit(solution)/shard_map/ppermute | solution.py:334
  5.6 11.1 %collective-permute-start.1 = (f32[1,64,128]{2,1,0:T(8,128)S(1)}, f32[1,64,128]{2,1,0:T(8,128)S(1)}, u32[]{:S(2)}, u32[]{:S(2)}) collective-permute-start(f32[1,64,128]{2,1,0:T(8,128)S(1)} %get-tuple-element.45), channel_id=1, source_target_pairs={{4,0},{8,4},{12,8},{16,12},{20,16},{24,20},{28,24},{0,28},{5,1},{9... | collective-permute-start | bytes 98312 | tf_op jit(solution)/shard_map/ppermute | solution.py:335
  10.3 12.6 %collective-permute-start.4 = (f32[66,1,128]{2,1,0:T(1,128)S(1)}, f32[66,1,128]{2,1,0:T(1,128)S(1)}, u32[]{:S(2)}, u32[]{:S(2)}) collective-permute-start(f32[66,1,128]{2,1,0:T(1,128)S(1)} %get-tuple-element.34), channel_id=1, source_target_pairs={{1,0},{2,1},{3,2},{5,4},{6,5},{7,6},{9,8},{10,9},{11,10},{13,12},{... | collective-permute-start | bytes 101384 | tf_op jit(solution)/shard_map/ppermute | solution.py:335
  11.6 11.3 %collective-permute-start.6 = (f32[66,1,128]{2,1,0:T(1,128)S(1)}, f32[66,1,128]{2,1,0:T(1,128)S(1)}, u32[]{:S(2)}, u32[]{:S(2)}) collective-permute-start(f32[66,1,128]{2,1,0:T(1,128)S(1)} %get-tuple-element.33), channel_id=1, source_target_pairs={{0,1},{1,2},{2,3},{4,5},{5,6},{6,7},{8,9},{9,10},{10,11},{12,13},{... | collective-permute-start | bytes 101384 | tf_op jit(solution)/shard_map/ppermute | solution.py:334
  16.8 6.1 %collective-permute-start.5 = (f32[66,1,128]{2,1,0:T(1,128)S(1)}, f32[66,1,128]{2,1,0:T(1,128)S(1)}, u32[]{:S(2)}, u32[]{:S(2)}) collective-permute-start(f32[66,1,128]{2,1,0:T(1,128)S(1)} %get-tuple-element.35), channel_id=1, source_target_pairs={{1,0},{2,1},{3,2},{5,4},{6,5},{7,6},{9,8},{10,9},{11,10},{13,12},{... | collective-permute-start | bytes 101384 | tf_op jit(solution)/shard_map/ppermute | solution.py:335
  18.4 6.1 %collective-permute-start.7 = (f32[66,1,128]{2,1,0:T(1,128)S(1)}, f32[66,1,128]{2,1,0:T(1,128)S(1)}, u32[]{:S(2)}, u32[]{:S(2)}) collective-permute-start(f32[66,1,128]{2,1,0:T(1,128)S(1)} %get-tuple-element.36), channel_id=1, source_target_pairs={{0,1},{1,2},{2,3},{4,5},{5,6},{6,7},{8,9},{9,10},{10,11},{12,13},{... | collective-permute-start | bytes 101384 | tf_op jit(solution)/shard_map/ppermute | solution.py:334
  32.4 29.9 %copy-start.4 = (f32[64,64,128]{2,1,0:T(8,128)}, f32[64,64,128]{2,1,0:T(8,128)S(1)}, u32[]{:S(2)}) copy-start(f32[64,64,128]{2,1,0:T(8,128)S(1)} %get-tuple-element.23) | copy-start | bytes 6291460
  32.4 29.9 %copy-start.5 = (f32[64,64,128]{2,1,0:T(8,128)}, f32[64,64,128]{2,1,0:T(8,128)S(1)}, u32[]{:S(2)}) copy-start(f32[64,64,128]{2,1,0:T(8,128)S(1)} %get-tuple-element.24) | copy-start | bytes 6291460
  32.4 29.9 %copy-start.6 = (f32[64,64,128]{2,1,0:T(8,128)}, f32[64,64,128]{2,1,0:T(8,128)S(1)}, u32[]{:S(2)}) copy-start(f32[64,64,128]{2,1,0:T(8,128)S(1)} %get-tuple-element.25) | copy-start | bytes 6291460
  32.4 1.7 collective-permute-start.8
  32.5 4.3 %collective-permute-start.9 = (f32[1,64,128]{2,1,0:T(8,128)S(1)}, f32[1,64,128]{2,1,0:T(8,128)S(1)}, u32[]{:S(2)}, u32[]{:S(2)}) collective-permute-start(f32[1,64,128]{2,1,0:T(8,128)S(1)} %get-tuple-element.41), channel_id=1, source_target_pairs={{0,4},{4,8},{8,12},{12,16},{16,20},{20,24},{24,28},{28,0},{1,5},{5... | collective-permute-start | bytes 98312 | tf_op jit(solution)/shard_map/ppermute | solution.py:334
  36.8 6.2 %collective-permute-start.10 = (f32[66,1,128]{2,1,0:T(1,128)S(1)}, f32[66,1,128]{2,1,0:T(1,128)S(1)}, u32[]{:S(2)}, u32[]{:S(2)}) collective-permute-start(f32[66,1,128]{2,1,0:T(1,128)S(1)} %get-tuple-element.31), channel_id=1, source_target_pairs={{1,0},{2,1},{3,2},{5,4},{6,5},{7,6},{9,8},{10,9},{11,10},{13,12},{... | collective-permute-start | bytes 101384 | tf_op jit(solution)/shard_map/ppermute | solution.py:335
  38.1 6.4 %collective-permute-start.11 = (f32[66,1,128]{2,1,0:T(1,128)S(1)}, f32[66,1,128]{2,1,0:T(1,128)S(1)}, u32[]{:S(2)}, u32[]{:S(2)}) collective-permute-start(f32[66,1,128]{2,1,0:T(1,128)S(1)} %get-tuple-element.32), channel_id=1, source_target_pairs={{0,1},{1,2},{2,3},{4,5},{5,6},{6,7},{8,9},{9,10},{10,11},{12,13},{... | collective-permute-start | bytes 101384 | tf_op jit(solution)/shard_map/ppermute | solution.py:334
  50.1 1.7 collective-permute-start.12
  50.2 4.3 %collective-permute-start.13 = (f32[1,64,128]{2,1,0:T(8,128)S(1)}, f32[1,64,128]{2,1,0:T(8,128)S(1)}, u32[]{:S(2)}, u32[]{:S(2)}) collective-permute-start(f32[1,64,128]{2,1,0:T(8,128)S(1)} %get-tuple-element.39), channel_id=1, source_target_pairs={{0,4},{4,8},{8,12},{12,16},{16,20},{20,24},{24,28},{28,0},{1,5},{5... | collective-permute-start | bytes 98312 | tf_op jit(solution)/shard_map/ppermute | solution.py:334
  54.5 6.2 %collective-permute-start.14 = (f32[66,1,128]{2,1,0:T(1,128)S(1)}, f32[66,1,128]{2,1,0:T(1,128)S(1)}, u32[]{:S(2)}, u32[]{:S(2)}) collective-permute-start(f32[66,1,128]{2,1,0:T(1,128)S(1)} %get-tuple-element.29), channel_id=1, source_target_pairs={{1,0},{2,1},{3,2},{5,4},{6,5},{7,6},{9,8},{10,9},{11,10},{13,12},{... | collective-permute-start | bytes 101384 | tf_op jit(solution)/shard_map/ppermute | solution.py:335
  55.8 6.4 %collective-permute-start.15 = (f32[66,1,128]{2,1,0:T(1,128)S(1)}, f32[66,1,128]{2,1,0:T(1,128)S(1)}, u32[]{:S(2)}, u32[]{:S(2)}) collective-permute-start(f32[66,1,128]{2,1,0:T(1,128)S(1)} %get-tuple-element.30), channel_id=1, source_target_pairs={{0,1},{1,2},{2,3},{4,5},{5,6},{6,7},{8,9},{9,10},{10,11},{12,13},{... | collective-permute-start | bytes 101384 | tf_op jit(solution)/shard_map/ppermute | solution.py:334
  67.9 1.7 collective-permute-start.16
  67.9 4.3 %collective-permute-start.17 = (f32[1,64,128]{2,1,0:T(8,128)S(1)}, f32[1,64,128]{2,1,0:T(8,128)S(1)}, u32[]{:S(2)}, u32[]{:S(2)}) collective-permute-start(f32[1,64,128]{2,1,0:T(8,128)S(1)} %get-tuple-element.37), channel_id=1, source_target_pairs={{0,4},{4,8},{8,12},{12,16},{16,20},{20,24},{24,28},{28,0},{1,5},{5... | collective-permute-start | bytes 98312 | tf_op jit(solution)/shard_map/ppermute | solution.py:334
  72.3 6.6 %collective-permute-start.18 = (f32[66,1,128]{2,1,0:T(1,128)S(1)}, f32[66,1,128]{2,1,0:T(1,128)S(1)}, u32[]{:S(2)}, u32[]{:S(2)}) collective-permute-start(f32[66,1,128]{2,1,0:T(1,128)S(1)} %get-tuple-element.27), channel_id=1, source_target_pairs={{1,0},{2,1},{3,2},{5,4},{6,5},{7,6},{9,8},{10,9},{11,10},{13,12},{... | collective-permute-start | bytes 101384 | tf_op jit(solution)/shard_map/ppermute | solution.py:335
  73.6 6.5 %collective-permute-start.19 = (f32[66,1,128]{2,1,0:T(1,128)S(1)}, f32[66,1,128]{2,1,0:T(1,128)S(1)}, u32[]{:S(2)}, u32[]{:S(2)}) collective-permute-start(f32[66,1,128]{2,1,0:T(1,128)S(1)} %get-tuple-element.28), channel_id=1, source_target_pairs={{0,1},{1,2},{2,3},{4,5},{5,6},{6,7},{8,9},{9,10},{10,11},{12,13},{... | collective-permute-start | bytes 101384 | tf_op jit(solution)/shard_map/ppermute | solution.py:334
  95.8 93.0 %copy-start = (f32[64,64,128]{2,1,0:T(8,128)}, f32[64,64,128]{2,1,0:T(8,128)S(1)}, u32[]{:S(2)}) copy-start(f32[64,64,128]{2,1,0:T(8,128)S(1)} %fusion.29.t_ref) | copy-start | bytes 6291460
  (9 other events, 94.1 us)

commit v2 on v1

--- a/solution.py
+++ b/solution.py
@@ -63,7 +63,8 @@
 
 
 class Comm:
-    def __init__(self, nl, nz, send_sem, recv_sem):
+    def __init__(self, nl, nz, send_sem, recv_sem, halo_send, halo_recv):
+        self.halo_send, self.halo_recv = halo_send, halo_recv
         self.nl, self.nz = nl, nz
         self.lon = lax.axis_index("lon")
         self.lat = lax.axis_index("lat")
@@ -102,6 +103,18 @@
             )
         return waits
 
+    def send(self, axis, shift, k, lane, source, target):
+        count = self.nl if axis == "lon" else self.nz
+        me = self.lon if axis == "lon" else self.lat
+        return pltpu.make_async_remote_copy(
+            src_ref=source,
+            dst_ref=target,
+            send_sem=self.halo_send.at[k, lane],
+            recv_sem=self.halo_recv.at[k, lane],
+            device_id={axis: lax.rem(me + shift + count, count)},
+            device_id_type=pl.DeviceIdType.MESH,
+        )
+
     def gather(self, axis, slots):
         me = self.lon if axis == "lon" else self.lat
         return self.start(axis, lambda peer: slots.at[me], lambda owner: slots.at[owner])
@@ -142,13 +155,120 @@
     comm.wait(third)
 
 
-def sweep_kernel(nl, nz, t_ref, u_ref, v_ref, w_ref,
-                 err_ref, lon_ref, lat_ref, rad_ref, core_ref,
-                 z1, x3, y3, f_ref, y1, y2, small,
+def harmonic(cond_a, cond_b):
+    summed = cond_a + cond_b
+    return 2.0 * cond_a * cond_b / jnp.where(summed > 0.0, summed, 1.0)
+
+
+def conduct(comm, t0, k_ref, q_ref, tb, hx, hy, hz, edge_k, hal_lon, hal_lat, pack):
+    ni, nj, nr = t0.shape
+    last_step = STEPS
+    has_lo, has_hi = comm.lat > 0, comm.lat < comm.nz - 1
+
+    def exchange(k, src):
+        lon_copies = (
+            comm.send("lon", 1, k, 0, src.at[ni - 1], hal_lon.at[k, 0]),
+            comm.send("lon", -1, k, 1, src.at[0], hal_lon.at[k, 1]),
+        )
+        lat_copies = (
+            (has_hi, has_lo, comm.send("lat", 1, k, 2, pack.at[k, 1], hal_lat.at[k, 0])),
+            (has_lo, has_hi, comm.send("lat", -1, k, 3, pack.at[k, 0], hal_lat.at[k, 1])),
+        )
+        for c in lon_copies:
+            c.start()
+        for out, _, c in lat_copies:
+            pl.when(out)(c.start)
+
+        def wait():
+            for c in lon_copies:
+                c.wait_recv()
+            for _, into, c in lat_copies:
+                pl.when(into)(c.wait_recv)
+
+        def wait_sent():
+            for c in lon_copies:
+                c.wait_send()
+            for out, _, c in lat_copies:
+                pl.when(out)(c.wait_send)
+
+        return wait, wait_sent
+
+    @pl.when(comm.lat == 0)
+    def _():
+        for k in range(STEPS + 1):
+            hal_lat[k, 0] = jnp.zeros((ni, nr), F32)
+
+    @pl.when(comm.lat == comm.nz - 1)
+    def _():
+        for k in range(STEPS + 1):
+            hal_lat[k, 1] = jnp.zeros((ni, nr), F32)
+
+    pack[last_step, 0] = k_ref[:, 0, :]
+    pack[last_step, 1] = k_ref[:, nj - 1, :]
+    pack[0, 0] = t0[:, 0, :]
+    pack[0, 1] = t0[:, nj - 1, :]
+    wait_k, sent_k = exchange(last_step, k_ref)
+    wait_t, sent_t = exchange(0, t0)
+
+    row = lax.broadcasted_iota(jnp.int32, (nj, nr), 0)
+    col = lax.broadcasted_iota(jnp.int32, (nj, nr), 1)
+
+    def faces(i):
+        k = k_ref[i]
+        hy[i] = jnp.where(row == 0, 0.0, harmonic(k, pltpu.roll(k, 1, 0)))
+        hz[i] = jnp.where(col == 0, 0.0, harmonic(k, pltpu.roll(k, 1, 1)))
+
+    @pl.loop(1, ni)
+    def _(i):
+        faces(i)
+        hx[i] = harmonic(k_ref[i], k_ref[i - 1])
+
+    faces(0)
+    wait_k()
+    hx[0] = harmonic(k_ref[0], hal_lon[last_step, 0])
+    hx[ni] = harmonic(k_ref[ni - 1], hal_lon[last_step, 1])
+    edge_k[0] = harmonic(pack[last_step, 0], hal_lat[last_step, 0])
+    edge_k[1] = harmonic(pack[last_step, 1], hal_lat[last_step, 1])
+
+    def slab(i, before, here, after):
+        fx = hx[i + 1] * (after - here) - hx[i] * (here - before)
+        fy = hy[i] * (here - pltpu.roll(here, 1, 0))
+        fz = hz[i] * (here - pltpu.roll(here, 1, 1))
+        change = q_ref[i] + fx + (pltpu.roll(fy, nj - 1, 0) - fy) + (pltpu.roll(fz, nr - 1, 1) - fz)
+        return here + time_step * change
+
+    for step in range(STEPS):
+        src = t0 if step == 0 else tb.at[(step - 1) % 2]
+        dst = tb.at[step % 2]
+
+        @pl.loop(1, ni - 1)
+        def _(i):
+            dst[i] = slab(i, src[i - 1], src[i], src[i + 1])
+
+        wait_t()
+        dst[0] = slab(0, hal_lon[step, 0], src[0], src[1])
+        dst[ni - 1] = slab(ni - 1, src[ni - 2], src[ni - 1], hal_lon[step, 1])
+        for side, j in ((0, 0), (1, nj - 1)):
+            flux = edge_k[side] * (hal_lat[step, side] - pack[step, side])
+            edge = dst[:, j, :] + time_step * flux
+            dst[:, j, :] = edge
+            if step < STEPS - 1:
+                pack[step + 1, side] = edge
+        sent_t()
+        if step < STEPS - 1:
+            wait_t, sent_t = exchange(step + 1, dst)
+    sent_k()
+
+
+def sweep_kernel(nl, nz, t0, k_ref, q_ref, u_ref, v_ref, w_ref,
+                 temp_ref, x3, lon_ref, lat_ref, rad_ref, core_ref,
+                 tb, hx, hy, hz, edge_k, hal_lon, hal_lat, pack,
+                 z1, y3, f_ref, y1, y2, small,
                  b1s, b2s, b3l, b3z, g1s, g2s, bufs, rss, zss, ags,
-                 send_sem, recv_sem):
-    comm = Comm(nl, nz, send_sem, recv_sem)
-    ni, nj, nr = t_ref.shape
+                 send_sem, recv_sem, halo_send, halo_recv, out_sem):
+    comm = Comm(nl, nz, send_sem, recv_sem, halo_send, halo_recv)
+    ni, nj, nr = t0.shape
+    t_ref = tb.at[(STEPS - 1) % 2]
     r = u_ref.shape[1]
     group = 128 // r
     blocks = r // group
@@ -161,6 +281,11 @@
         pl.semaphore_signal(barrier, inc=1, device_id={"lat": lax.rem(comm.lat + d, nz)},
                             device_id_type=pl.DeviceIdType.MESH)
 
+    pl.semaphore_wait(barrier, nl + nz - 2)
+    conduct(comm, t0, k_ref, q_ref, tb, hx, hy, hz, edge_k, hal_lon, hal_lat, pack)
+    out_copy = pltpu.make_async_copy(t_ref, temp_ref, out_sem)
+    out_copy.start()
+
     wt = w_ref[...].T
     wts = split(wt)
     ut = u_ref[...].T
@@ -181,8 +306,6 @@
             out = jnp.where(lane(ni) == g, dot3(split(z1[m * group + g]), v4), out)
         y1[m] = out
         bufs[0, pl.ds(m * r, r), :] = dot3(uts, split(out))
-
-    pl.semaphore_wait(barrier, nl + nz - 2)
 
     all_reduce(comm, bufs.at[0], rss.at[0], zss.at[0], ags.at[0])
 
@@ -278,20 +401,28 @@
         core_ref[pl.ds(m * 128, 128), :] = core.T
         f_ref[pl.ds(m * per, per)] = dot3(split(core), radh, TN).reshape(per, r, nr)
     lonb = split(lon_ref[...])
-    latb = split(lat_ref[...])
     for b in range(r):
         x3[:, b, :] = dot3(lonb, split(f_ref[:, b, :]))
-
-    @pl.loop(0, ni // 8)
-    def _(step):
-        for k in range(8):
-            i = step * 8 + k
-            err_ref[i] = t_ref[i] - dot3(latb, split(x3[i]))
-
+    out_copy.wait()
     comm.finish()
 
 
-def sweep(t, u, v, w):
+def error_kernel(t_ref, s_ref, lon_ref, lat_ref, rad_ref, core_ref,
+                 temp_out, err_out, lon_out, lat_out, rad_out, core_out):
+    latb = split(lat_ref[...])
+    for i in range(t_ref.shape[0]):
+        err_out[i] = t_ref[i] - dot3(latb, split(s_ref[i]))
+    temp_out[...] = t_ref[...]
+
+    @pl.when(pl.program_id(0) == 0)
+    def _():
+        lon_out[...] = lon_ref[...]
+        lat_out[...] = lat_ref[...]
+        rad_out[...] = rad_ref[...]
+        core_out[...] = core_ref[...]
+
+
+def local(t, k, q, u, v, w):
     nl, nz = lax.axis_size("lon"), lax.axis_size("lat")
     ni, nj, nr = t.shape
     r = u.shape[1]
@@ -303,73 +434,41 @@
     sds = lambda *s: jax.ShapeDtypeStruct(s, F32)
     V = lambda *s: pltpu.VMEM(s, F32)
     phases = 18
-    err, lon, lat, rad, core = pl.pallas_call(
+    small = (sds(ni, r), sds(nj, r), sds(nr, r), sds(r * r, r))
+    temp, s, lon, lat, rad, core = pl.pallas_call(
         functools.partial(sweep_kernel, nl, nz),
-        out_shape=(sds(ni, nj, nr), sds(ni, r), sds(nj, r), sds(nr, r), sds(r * r, r)),
-        in_specs=[vm] * 4,
-        out_specs=(vm,) * 5,
+        out_shape=(sds(ni, nj, nr), sds(ni, r, nr)) + small,
+        in_specs=[vm] * 6,
+        out_specs=(pl.BlockSpec(memory_space=pl.ANY),) + (vm,) * 5,
         scratch_shapes=[
-            V(r, ni, nj), V(ni, r, nr), V(r, r, nr), V(r, r, nr),
+            V(2, ni, nj, nr), V(ni + 1, nj, nr), V(ni, nj, nr), V(ni, nj, nr),
+            V(2, ni, nr), V(STEPS + 1, 2, nj, nr), V(STEPS + 1, 2, ni, nr), V(STEPS + 1, 2, ni, nr),
+            V(r, ni, nj), V(r, r, nr), V(r, r, nr),
             V(blocks, ni, 128), V(blocks, nj, 128), V(2, r, r),
             V(nz, r, ni), V(nl, r, nj), V(nl, r, nr), V(nz, r, nr),
             V(nl, r, r), V(nz, r, r),
             V(4, rows, 128), V(4, nl, piece, 128), V(4, nz, piece, 128), V(4, rows, 128),
             pltpu.SemaphoreType.DMA((phases, most)),
             pltpu.SemaphoreType.DMA((phases, most)),
+            pltpu.SemaphoreType.DMA((STEPS + 1, 4)),
+            pltpu.SemaphoreType.DMA((STEPS + 1, 4)),
+            pltpu.SemaphoreType.DMA,
         ],
         compiler_params=pltpu.CompilerParams(
-            collective_id=1, has_side_effects=True, vmem_limit_bytes=40 * 1024 * 1024
+            collective_id=1, has_side_effects=True, vmem_limit_bytes=48 * 1024 * 1024
         ),
-    )(t, u, v, w)
-    return err, lon, lat, rad, core.reshape(r, r, r)
-
-
-def extended(x, sides, width, wrap):
-    for axis, dim in sides:
-        count, length = (lax.axis_size(axis), x.shape[dim])
-        up = [(i, (i + 1) % count) for i in range(count if wrap else count - 1)]
-        down = [(j, i) for i, j in up]
-        last = lax.slice_in_dim(x, length - width, length, axis=dim)
-        initial = lax.slice_in_dim(x, 0, width, axis=dim)
-        before = lax.ppermute(last, axis, up)
-        after = lax.ppermute(initial, axis, down)
-        x = jnp.concatenate([before, x, after], axis=dim)
-    return x
-
-
-def harmonic(cond_a, cond_b):
-    summed = cond_a + cond_b
-    return 2.0 * cond_a * cond_b / jnp.where(summed > 0.0, summed, 1.0)
-
-
-def advance(padded, cond_pad, interior_power_source):
-    centre = padded[1:-1, 1:-1]
-    kcentre = cond_pad[1:-1, 1:-1]
-    change = interior_power_source
-    pairs = (
-        (padded[2:, 1:-1], cond_pad[2:, 1:-1]),
-        (padded[:-2, 1:-1], cond_pad[:-2, 1:-1]),
-        (padded[1:-1, 2:], cond_pad[1:-1, 2:]),
-        (padded[1:-1, :-2], cond_pad[1:-1, :-2]),
-    )
-    for near_t, near_k in pairs:
-        change = change + harmonic(kcentre, near_k) * (near_t - centre)
-    radial_t = jnp.pad(centre, ((0, 0), (0, 0), (1, 1)))
-    radial_k = jnp.pad(kcentre, ((0, 0), (0, 0), (1, 1)))
-    change = change + harmonic(kcentre, radial_k[:, :, 2:]) * (radial_t[:, :, 2:] - centre)
-    change = change + harmonic(kcentre, radial_k[:, :, :-2]) * (radial_t[:, :, :-2] - centre)
-    return centre + time_step * change
-
-
-def local(temp, cond, source, lon_basis, lat_basis, rad_basis):
-    cond_lon = extended(cond, (("lon", 0),), 1, True)
-    cond_pad = extended(cond_lon, (("lat", 1),), 1, False)
-    for _ in range(STEPS):
-        temp_lon = extended(temp, (("lon", 0),), 1, True)
-        padded = extended(temp_lon, (("lat", 1),), 1, False)
-        temp = advance(padded, cond_pad, source)
-    err, lon, lat, rad, core = sweep(temp, lon_basis, lat_basis, rad_basis)
-    return temp, err, lon, lat, rad, core
+    )(t, k, q, u, v, w)
+    at = 8
+    slabs = lambda n: pl.BlockSpec((at, n, nr), lambda i: (i, 0, 0))
+    whole = [pl.BlockSpec(x.shape, lambda i: (0, 0)) for x in small]
+    temp, err, lon, lat, rad, core = pl.pallas_call(
+        error_kernel,
+        grid=(ni // at,),
+        out_shape=(sds(ni, nj, nr), sds(ni, nj, nr)) + small,
+        in_specs=[slabs(nj), slabs(r)] + whole,
+        out_specs=[slabs(nj), slabs(nj)] + whole,
+    )(temp, s, lon, lat, rad, core)
+    return temp, err, lon, lat, rad, core.reshape(r, r, r)
 
 
 def solution(mesh):

time: 190 us -> 155 us (0.82)
  Pallas kernels: 86.4 us -> 141 us
  starting transfers between devices: 38.6 us -> 0 us
  other arithmetic: 34.7 us -> 0 us
  waiting for transfers between devices: 17.2 us -> 0 us
    pallas_call x1 -> x2, Pallas kernels: 86.4 us -> 141 us  [the longest x1 133 us: local(): pl.pallas_call(functools.partial(sweep_kernel, nl, nz), out_shape=(sds(ni...]
    ppermute x20 -> x0, starting transfers between devices: 38.6 us -> none  [the longest x10 26.1 us: extended(): before = lax.ppermute(last, axis, up)]
    add x4 -> x0, other arithmetic: 34.5 us -> none  [advance(): return centre + time_step * change]
    ppermute x20 -> x0, waiting for transfers between devices: 17.2 us -> none  [the longest x10 13.9 us: extended(): before = lax.ppermute(last, axis, up)]
    unnamed x38 -> x20, local copies, waits for them, and re-layouts: 9.88 us -> 13.3 us
  transfers between devices with their start and end apart: 20 -> 0, of which waited for: 10 -> 0; matrix products, arithmetic and copies ran while one was open for 2% -> 0% of each run, Pallas kernels for 0% -> 0%
where the time goes in v2:
time: 155 us
  Pallas kernels  141 us (91%)
  local copies, waits for them, and re-layouts  13.3 us (9%)
    pallas_call x1, Pallas kernels, local(): pl.pallas_call(functools.partial(sweep_kernel, nl, nz), out_shape=(sds(ni...  133 us
    unnamed x20, local copies, waits for them, and re-layouts  13.3 us
    pallas_call x1, Pallas kernels, local(): pl.pallas_call(error_kernel, grid=(ni // at,), out_shape=(sds(ni, nj, nr)...  7.64 us

profile of v2, /device:TPU:0, one launch (start us, length us, event | category | flops | bytes accessed | tf_op | source)
XLA Modules:
  0.0 154.8 jit_solution(7095644417493962802)
XLA Ops:
  0.6 0.8 copy.12.u_ref
  1.4 0.8 copy.13.v_ref
  2.2 0.8 copy.14.w_ref
  3.0 0.0 copy-start
  3.1 1.6 %copy-done = f32[64,64,128]{2,1,0:T(8,128)S(1)} copy-done((f32[64,64,128]{2,1,0:T(8,128)S(1)}, f32[64,64,128]{2,1,0:T(8,128)}, u32[]{:S(2)}) %copy-start) | copy-done | bytes 2097176
  4.6 133.2 %shard_map.109 = (f32[64,64,128]{2,1,0:T(8,128)S(1)}, f32[64,32,128]{2,1,0:T(8,128)S(1)}, f32[64,32]{1,0:T(8,128)S(1)}, f32[64,32]{1,0:T(8,128)S(1)}, f32[128,32]{1,0:T(8,128)S(1)}, /*index=5*/f32[1024,32]{1,0:T(8,128)S(1)}) custom-call(f32[64,64,128]{2,1,0:T(8,128)S(1)} %copy-done, f32[64,64,128]{2,1,0:T(8,128)} %k_ref.1, f32[64,64,128]{2,1,0:T(8,128)} %q_ref.1, ...), custom_call_target="tpu_custom_call" | custom-call | tf_op jit(solution)/shard_map/pallas_call | solution.py:438
  137.8 0.0 copy-start.1
  137.8 1.3 copy-done.1
  139.2 0.0 copy-start.2
  139.2 1.0 copy-done.2
  140.2 0.0 copy-start.3
  140.2 0.8 copy-done.3
  141.0 0.0 copy-start.4
  141.0 0.6 copy-done.4
  141.6 0.0 copy-start.5
  141.6 0.6 copy-done.5
  142.2 0.0 copy-start.6
  142.2 0.6 copy-done.6
  142.8 7.6 %shard_map.110 = (f32[64,64,128]{2,1,0:T(8,128)}, f32[64,64,128]{2,1,0:T(8,128)}, f32[64,32]{1,0:T(8,128)}, f32[64,32]{1,0:T(8,128)}, f32[128,32]{1,0:T(8,128)}, /*index=5*/f32[1024,32]{1,0:T(8,128)}) custom-call(f32[64,64,128]{2,1,0:T(8,128)} %copy-done.1, f32[64,32,128]{2,1,0:T(8,128)} %copy-done.2, f32[64,32]{1,0:T(8,128)} %copy-done.5, ...), custom_call_target="tpu_custom_call" | custom-call | tf_op jit(solution)/shard_map/pallas_call | solution.py:464
  150.4 1.4 copy.15
  151.9 1.4 copy.16
  153.3 1.5 copy.17
Async XLA Ops:
  3.0 1.6 %copy-start = (f32[64,64,128]{2,1,0:T(8,128)S(1)}, f32[64,64,128]{2,1,0:T(8,128)}, u32[]{:S(2)}) copy-start(f32[64,64,128]{2,1,0:T(8,128)} %t0.1) | copy-start | bytes 6291460
  137.8 1.3 copy-start.1
  139.2 1.0 copy-start.2
  140.2 0.8 copy-start.3
  141.0 0.6 copy-start.4
  141.6 0.6 copy-start.5
  142.2 0.6 copy-start.6

commit v3 on v2

--- a/solution.py
+++ b/solution.py
@@ -160,7 +160,31 @@
     return 2.0 * cond_a * cond_b / jnp.where(summed > 0.0, summed, 1.0)
 
 
-def conduct(comm, t0, k_ref, q_ref, tb, hx, hy, hz, edge_k, hal_lon, hal_lat, pack):
+def batched(low, high, size, values, store):
+    def group(first, count):
+        outs = [values(first + k) for k in range(count)]
+        for k, out in enumerate(outs):
+            store(first + k, out)
+
+    trips = (high - low) // size
+
+    @pl.loop(0, trips)
+    def _(trip):
+        group(low + trip * size, size)
+
+    left = high - low - trips * size
+    if left:
+        group(high - left, left)
+
+
+def store_in(ref):
+    def store(i, value):
+        ref[i] = value
+
+    return store
+
+
+def conduct(comm, t0, k_ref, q_ref, ta, tb, hx, hy, hz, edge_k, hal_lon, hal_lat, pack):
     ni, nj, nr = t0.shape
     last_step = STEPS
     has_lo, has_hi = comm.lat > 0, comm.lat < comm.nz - 1
@@ -215,15 +239,16 @@
 
     def faces(i):
         k = k_ref[i]
-        hy[i] = jnp.where(row == 0, 0.0, harmonic(k, pltpu.roll(k, 1, 0)))
-        hz[i] = jnp.where(col == 0, 0.0, harmonic(k, pltpu.roll(k, 1, 1)))
-
-    @pl.loop(1, ni)
-    def _(i):
-        faces(i)
-        hx[i] = harmonic(k_ref[i], k_ref[i - 1])
-
-    faces(0)
+        return (
+            jnp.where(row == 0, 0.0, harmonic(k, pltpu.roll(k, 1, 0))),
+            jnp.where(col == 0, 0.0, harmonic(k, pltpu.roll(k, 1, 1))),
+        )
+
+    def store_faces(i, values):
+        hy[i], hz[i] = values
+
+    batched(0, ni, 2, faces, store_faces)
+    batched(1, ni, 4, lambda i: harmonic(k_ref[i], k_ref[i - 1]), store_in(hx))
     wait_k()
     hx[0] = harmonic(k_ref[0], hal_lon[last_step, 0])
     hx[ni] = harmonic(k_ref[ni - 1], hal_lon[last_step, 1])
@@ -238,12 +263,10 @@
         return here + time_step * change
 
     for step in range(STEPS):
-        src = t0 if step == 0 else tb.at[(step - 1) % 2]
-        dst = tb.at[step % 2]
-
-        @pl.loop(1, ni - 1)
-        def _(i):
-            dst[i] = slab(i, src[i - 1], src[i], src[i + 1])
+        src = t0 if step == 0 else (ta, tb)[(step - 1) % 2]
+        dst = (ta, tb)[step % 2]
+
+        batched(1, ni - 1, 4, lambda i: slab(i, src[i - 1], src[i], src[i + 1]), store_in(dst))
 
         wait_t()
         dst[0] = slab(0, hal_lon[step, 0], src[0], src[1])
@@ -262,14 +285,14 @@
 
 def sweep_kernel(nl, nz, t0, k_ref, q_ref, u_ref, v_ref, w_ref,
                  temp_ref, x3, lon_ref, lat_ref, rad_ref, core_ref,
-                 tb, hx, hy, hz, edge_k, hal_lon, hal_lat, pack,
+                 ta, tb, hx, hy, hz, edge_k, hal_lon, hal_lat, pack,
                  z1, y3, f_ref, y1, y2, small,
                  b1s, b2s, b3l, b3z, g1s, g2s, bufs, rss, zss, ags,
                  send_sem, recv_sem, halo_send, halo_recv, out_sem):
     comm = Comm(nl, nz, send_sem, recv_sem, halo_send, halo_recv)
     ni, nj, nr = t0.shape
-    t_ref = tb.at[(STEPS - 1) % 2]
-    r = u_ref.shape[1]
+    t_ref = (ta, tb)[(STEPS - 1) % 2]
+    r = u_ref.shape[0]
     group = 128 // r
     blocks = r // group
 
@@ -282,23 +305,21 @@
                             device_id_type=pl.DeviceIdType.MESH)
 
     pl.semaphore_wait(barrier, nl + nz - 2)
-    conduct(comm, t0, k_ref, q_ref, tb, hx, hy, hz, edge_k, hal_lon, hal_lat, pack)
+    conduct(comm, t0, k_ref, q_ref, ta, tb, hx, hy, hz, edge_k, hal_lon, hal_lat, pack)
     out_copy = pltpu.make_async_copy(t_ref, temp_ref, out_sem)
     out_copy.start()
 
-    wt = w_ref[...].T
-    wts = split(wt)
-    ut = u_ref[...].T
-    vt = v_ref[...].T
-
-    @pl.loop(0, ni // 8)
-    def _(step):
-        for k in range(8):
-            i = step * 8 + k
-            z1[:, i, :] = dot3(wts, split(t_ref[i]), NT)
+    wts = split(w_ref[...])
+    ut = u_ref[...]
+    vt = v_ref[...]
+
+    def store_z1(i, value):
+        z1[:, i, :] = value
+
+    batched(0, ni, 8, lambda i: dot3(wts, split(t_ref[i]), NT), store_z1)
 
     lane = lambda n: lax.broadcasted_iota(jnp.int32, (n, 128), 1) // r
-    v4 = split(jnp.concatenate([v_ref[...]] * group, axis=1))
+    v4 = split(jnp.concatenate([vt.T] * group, axis=1))
     uts = split(ut)
     for m in range(blocks):
         out = jnp.zeros((ni, 128), F32)
@@ -342,18 +363,14 @@
     b2s[comm.lon] = acc
     w = comm.gather("lon", b2s)
     lont = mmh(l1, b1t)
-    lon_ref[...] = lont.T
+    lon_ref[...] = lont
     comm.wait(w)
     b2t = total(b2s)
     g2s[comm.lat] = mmh(b2t, b2t, NT)
     g2w = comm.gather("lat", g2s)
     b2h = split(b2t)
 
-    @pl.loop(0, ni // 8)
-    def _(step):
-        for k in range(8):
-            i = step * 8 + k
-            x3[i] = dot3(b2h, split(t_ref[i]))
+    batched(0, ni, 8, lambda i: dot3(b2h, split(t_ref[i])), store_in(x3))
 
     lonh = split(lont)
     for b in range(r):
@@ -381,7 +398,7 @@
     b3l[comm.lon] = acc
     w = comm.gather("lon", b3l)
     latt = mmh(l2, b2t)
-    lat_ref[...] = latt.T
+    lat_ref[...] = latt
     comm.wait(w)
     b3z[comm.lat] = total(b3l)
     w = comm.gather("lat", b3z)
@@ -389,7 +406,7 @@
     b3t = total(b3z)
     l3 = chol_inverse(mmh(b3t, b3t, NT))
     radt = mmh(l3, b3t)
-    rad_ref[...] = radt.T
+    rad_ref[...] = radt
     radh = split(radt)
     for m in range(blocks):
         bufs[3, pl.ds(m * r, r), :] = dot3(radh, y3block(m), NT)
@@ -400,7 +417,7 @@
         core = dot3(split(ags[3, pl.ds(m * r, r), :]), bdl)
         core_ref[pl.ds(m * 128, 128), :] = core.T
         f_ref[pl.ds(m * per, per)] = dot3(split(core), radh, TN).reshape(per, r, nr)
-    lonb = split(lon_ref[...])
+    lonb = split(lont.T)
     for b in range(r):
         x3[:, b, :] = dot3(lonb, split(f_ref[:, b, :]))
     out_copy.wait()
@@ -408,18 +425,34 @@
 
 
 def error_kernel(t_ref, s_ref, lon_ref, lat_ref, rad_ref, core_ref,
-                 temp_out, err_out, lon_out, lat_out, rad_out, core_out):
-    latb = split(lat_ref[...])
-    for i in range(t_ref.shape[0]):
-        err_out[i] = t_ref[i] - dot3(latb, split(s_ref[i]))
-    temp_out[...] = t_ref[...]
-
-    @pl.when(pl.program_id(0) == 0)
-    def _():
-        lon_out[...] = lon_ref[...]
-        lat_out[...] = lat_ref[...]
-        rad_out[...] = rad_ref[...]
-        core_out[...] = core_ref[...]
+                 temp_out, err_out, lon_out, lat_out, rad_out, core_out, err, sem, temp_sem):
+    temp_copy = pltpu.make_async_copy(t_ref, temp_out, temp_sem)
+    temp_copy.start()
+    latb = split(lat_ref[...].T)
+    ni = t_ref.shape[0]
+    at = 8
+
+    def chunk(c):
+        part = pl.ds(c * at, at)
+        return pltpu.make_async_copy(err.at[part], err_out.at[part], sem.at[c])
+
+    @pl.loop(0, ni // at)
+    def _(c):
+        outs = [t_ref[c * at + k] - dot3(latb, split(s_ref[c * at + k])) for k in range(at)]
+        for k, out in enumerate(outs):
+            err[c * at + k] = out
+        chunk(c).start()
+
+    lon_out[...] = lon_ref[...]
+    lat_out[...] = lat_ref[...]
+    rad_out[...] = rad_ref[...]
+    core_out[...] = core_ref[...]
+
+    @pl.loop(0, ni // at)
+    def _(c):
+        chunk(c).wait()
+
+    temp_copy.wait()
 
 
 def local(t, k, q, u, v, w):
@@ -434,14 +467,14 @@
     sds = lambda *s: jax.ShapeDtypeStruct(s, F32)
     V = lambda *s: pltpu.VMEM(s, F32)
     phases = 18
-    small = (sds(ni, r), sds(nj, r), sds(nr, r), sds(r * r, r))
+    small = (sds(r, ni), sds(r, nj), sds(r, nr), sds(r * r, r))
     temp, s, lon, lat, rad, core = pl.pallas_call(
         functools.partial(sweep_kernel, nl, nz),
         out_shape=(sds(ni, nj, nr), sds(ni, r, nr)) + small,
         in_specs=[vm] * 6,
         out_specs=(pl.BlockSpec(memory_space=pl.ANY),) + (vm,) * 5,
         scratch_shapes=[
-            V(2, ni, nj, nr), V(ni + 1, nj, nr), V(ni, nj, nr), V(ni, nj, nr),
+            V(ni, nj, nr), V(ni, nj, nr), V(ni + 1, nj, nr), V(ni, nj, nr), V(ni, nj, nr),
             V(2, ni, nr), V(STEPS + 1, 2, nj, nr), V(STEPS + 1, 2, ni, nr), V(STEPS + 1, 2, ni, nr),
             V(r, ni, nj), V(r, r, nr), V(r, r, nr),
             V(blocks, ni, 128), V(blocks, nj, 128), V(2, r, r),
@@ -457,18 +490,19 @@
         compiler_params=pltpu.CompilerParams(
             collective_id=1, has_side_effects=True, vmem_limit_bytes=48 * 1024 * 1024
         ),
-    )(t, k, q, u, v, w)
-    at = 8
-    slabs = lambda n: pl.BlockSpec((at, n, nr), lambda i: (i, 0, 0))
-    whole = [pl.BlockSpec(x.shape, lambda i: (0, 0)) for x in small]
+    )(t, k, q, u.T, v.T, w.T)
+    anywhere = pl.BlockSpec(memory_space=pl.ANY)
     temp, err, lon, lat, rad, core = pl.pallas_call(
         error_kernel,
-        grid=(ni // at,),
         out_shape=(sds(ni, nj, nr), sds(ni, nj, nr)) + small,
-        in_specs=[slabs(nj), slabs(r)] + whole,
-        out_specs=[slabs(nj), slabs(nj)] + whole,
+        in_specs=[vm] * 6,
+        out_specs=(anywhere, anywhere) + (vm,) * 4,
+        scratch_shapes=[
+            V(ni, nj, nr), pltpu.SemaphoreType.DMA((ni // 8,)), pltpu.SemaphoreType.DMA
+        ],
+        compiler_params=pltpu.CompilerParams(vmem_limit_bytes=12 * 1024 * 1024),
     )(temp, s, lon, lat, rad, core)
-    return temp, err, lon, lat, rad, core.reshape(r, r, r)
+    return temp, err, lon.T, lat.T, rad.T, core.reshape(r, r, r)
 
 
 def solution(mesh):

time: 155 us -> 114 us (0.74)
  Pallas kernels: 141 us -> 109 us
  local copies, waits for them, and re-layouts: 13.3 us -> 3.73 us
    pallas_call x1, Pallas kernels: 133 us -> 106 us  [local(): pl.pallas_call(functools.partial(sweep_kernel, nl, nz), out_shape=(sds(ni...]
    unnamed x20 -> x8, local copies, waits for them, and re-layouts: 13.3 us -> 3.73 us
    pallas_call x1, Pallas kernels: 7.64 us -> 3.71 us  [local(): pl.pallas_call(error_kernel, out_shape=(sds(ni, nj, nr), sds(ni, nj, nr))...]
where the time goes in v3:
time: 114 us
  Pallas kernels  109 us (96%)
  local copies, waits for them, and re-layouts  3.73 us (3%)
    pallas_call x1, Pallas kernels, local(): pl.pallas_call(functools.partial(sweep_kernel, nl, nz), out_shape=(sds(ni...  106 us
    unnamed x8, local copies, waits for them, and re-layouts  3.73 us
    pallas_call x1, Pallas kernels, local(): pl.pallas_call(error_kernel, out_shape=(sds(ni, nj, nr), sds(ni, nj, nr))...  3.71 us

profile of v3, /device:TPU:0, one launch (start us, length us, event | category | flops | bytes accessed | tf_op | source)
XLA Modules:
  0.0 113.9 jit_solution(28851566197740406)
XLA Ops:
  0.6 0.0 copy-start
  0.6 1.6 %copy-done = f32[64,64,128]{2,1,0:T(8,128)S(1)} copy-done((f32[64,64,128]{2,1,0:T(8,128)S(1)}, f32[64,64,128]{2,1,0:T(8,128)}, u32[]{:S(2)}) %copy-start) | copy-done | bytes 2097176
  2.2 0.0 copy-start.1
  2.2 0.7 copy-done.1
  2.9 0.0 copy-start.2
  2.9 0.7 copy-done.2
  3.7 0.0 copy-start.3
  3.7 0.7 copy-done.3
  4.4 105.6 %shard_map.109 = (f32[64,64,128]{2,1,0:T(8,128)S(1)}, f32[64,32,128]{2,1,0:T(8,128)S(1)}, f32[32,64]{1,0:T(8,128)S(1)}, f32[32,64]{1,0:T(8,128)S(1)}, f32[32,128]{1,0:T(8,128)S(1)}, /*index=5*/f32[1024,32]{1,0:T(8,128)S(1)}) custom-call(f32[64,64,128]{2,1,0:T(8,128)S(1)} %copy-done, f32[64,64,128]{2,1,0:T(8,128)} %k_ref.1, f32[64,64,128]{2,1,0:T(8,128)} %q_ref.1, ...), custom_call_target="tpu_custom_call" | custom-call | tf_op jit(solution)/shard_map/pallas_call | solution.py:471
  110.0 3.7 %shard_map.110 = (f32[64,64,128]{2,1,0:T(8,128)}, f32[64,64,128]{2,1,0:T(8,128)}, f32[32,64]{1,0:T(8,128)}, f32[32,64]{1,0:T(8,128)}, f32[32,128]{1,0:T(8,128)}, /*index=5*/f32[1024,32]{1,0:T(8,128)}) custom-call(f32[64,64,128]{2,1,0:T(8,128)S(1)} %get-tuple-element.18.t_ref, f32[64,32,128]{2,1,0:T(8,128)S(1)} %get-tuple-element.19.s_ref, ...), custom_call_target="tpu_custom_call" | custom-call | tf_op jit(solution)/shard_map/pallas_call | solution.py:495
Async XLA Ops:
  0.6 1.6 %copy-start = (f32[64,64,128]{2,1,0:T(8,128)S(1)}, f32[64,64,128]{2,1,0:T(8,128)}, u32[]{:S(2)}) copy-start(f32[64,64,128]{2,1,0:T(8,128)} %t0.1) | copy-start | bytes 6291460
  2.2 0.7 copy-start.1
  2.9 0.7 copy-start.2
  3.7 0.7 copy-start.3

commit v4 on v3

--- a/solution.py
+++ b/solution.py
@@ -286,7 +286,7 @@
 def sweep_kernel(nl, nz, t0, k_ref, q_ref, u_ref, v_ref, w_ref,
                  temp_ref, x3, lon_ref, lat_ref, rad_ref, core_ref,
                  ta, tb, hx, hy, hz, edge_k, hal_lon, hal_lat, pack,
-                 z1, y3, f_ref, y1, y2, small,
+                 z1, z1t, y3h, y3, f_ref, y1, y2, small,
                  b1s, b2s, b3l, b3z, g1s, g2s, bufs, rss, zss, ags,
                  send_sem, recv_sem, halo_send, halo_recv, out_sem):
     comm = Comm(nl, nz, send_sem, recv_sem, halo_send, halo_recv)
@@ -328,7 +328,12 @@
         y1[m] = out
         bufs[0, pl.ds(m * r, r), :] = dot3(uts, split(out))
 
-    all_reduce(comm, bufs.at[0], rss.at[0], zss.at[0], ags.at[0])
+    def turn(low, high):
+        for b in range(low, high):
+            z1t[b] = z1[b].T
+
+    turns = tuple(functools.partial(turn, r * k // 3, r * (k + 1) // 3) for k in range(3))
+    all_reduce(comm, bufs.at[0], rss.at[0], zss.at[0], ags.at[0], turns)
 
     acc = jnp.zeros((r, ni), F32)
     for m in range(blocks):
@@ -344,7 +349,7 @@
     for m in range(blocks):
         out = jnp.zeros((nj, 128), F32)
         for g in range(group):
-            out = jnp.where(lane(nj) == g, dot3(split(z1[m * group + g]), b1x, TN), out)
+            out = jnp.where(lane(nj) == g, dot3(split(z1t[m * group + g]), b1x), out)
         y2[m] = out
         bufs[1, pl.ds(m * r, r), :] = dot3(vts, split(out))
 
@@ -382,7 +387,13 @@
         return split(y3[pl.ds(m * per, per)].reshape(128, nr))
 
     for m in range(blocks):
-        bufs[2, pl.ds(m * r, r), :] = dot3(wts, y3block(m), NT)
+        high, low = y3block(m)
+        y3h[0, pl.ds(m * 128, 128), :] = high
+        y3h[1, pl.ds(m * 128, 128), :] = low
+        bufs[2, pl.ds(m * r, r), :] = dot3(wts, (high, low), NT)
+
+    def y3kept(m):
+        return y3h[0, pl.ds(m * 128, 128), :], y3h[1, pl.ds(m * 128, 128), :]
 
     def chol2():
         comm.wait(g2w)
@@ -394,7 +405,7 @@
     bd2 = split(block_diag(mmh(l2, l2, TN), group))
     acc = jnp.zeros((r, nr), F32)
     for m in range(blocks):
-        acc = acc + dot3(split(dot3(split(ags[2, pl.ds(m * r, r), :]), bd2)), y3block(m))
+        acc = acc + dot3(split(dot3(split(ags[2, pl.ds(m * r, r), :]), bd2)), y3kept(m))
     b3l[comm.lon] = acc
     w = comm.gather("lon", b3l)
     latt = mmh(l2, b2t)
@@ -409,7 +420,7 @@
     rad_ref[...] = radt
     radh = split(radt)
     for m in range(blocks):
-        bufs[3, pl.ds(m * r, r), :] = dot3(radh, y3block(m), NT)
+        bufs[3, pl.ds(m * r, r), :] = dot3(radh, y3kept(m), NT)
     all_reduce(comm, bufs.at[3], rss.at[3], zss.at[3], ags.at[3])
 
     bdl = split(block_diag(l2.T, group))
@@ -476,7 +487,7 @@
         scratch_shapes=[
             V(ni, nj, nr), V(ni, nj, nr), V(ni + 1, nj, nr), V(ni, nj, nr), V(ni, nj, nr),
             V(2, ni, nr), V(STEPS + 1, 2, nj, nr), V(STEPS + 1, 2, ni, nr), V(STEPS + 1, 2, ni, nr),
-            V(r, ni, nj), V(r, r, nr), V(r, r, nr),
+            V(r, ni, nj), V(r, nj, ni), pltpu.VMEM((2, r * r, nr), BF16), V(r, r, nr), V(r, r, nr),
             V(blocks, ni, 128), V(blocks, nj, 128), V(2, r, r),
             V(nz, r, ni), V(nl, r, nj), V(nl, r, nr), V(nz, r, nr),
             V(nl, r, r), V(nz, r, r),

time: 114 us -> 114 us (level)
  no operation moved by 1% of the time
where the time goes in v4:
time: 114 us
  Pallas kernels  109 us (96%)
  local copies, waits for them, and re-layouts  3.73 us (3%)
    pallas_call x1, Pallas kernels, local(): pl.pallas_call(functools.partial(sweep_kernel, nl, nz), out_shape=(sds(ni...  106 us
    unnamed x8, local copies, waits for them, and re-layouts  3.73 us
    pallas_call x1, Pallas kernels, local(): pl.pallas_call(error_kernel, out_shape=(sds(ni, nj, nr), sds(ni, nj, nr))...  3.71 us

profile of v4, /device:TPU:0, one launch (start us, length us, event | category | flops | bytes accessed | tf_op | source)
XLA Modules:
  0.0 113.8 jit_solution(15923732079209891919)
XLA Ops:
  0.6 0.0 copy-start
  0.6 1.6 %copy-done = f32[64,64,128]{2,1,0:T(8,128)S(1)} copy-done((f32[64,64,128]{2,1,0:T(8,128)S(1)}, f32[64,64,128]{2,1,0:T(8,128)}, u32[]{:S(2)}) %copy-start) | copy-done | bytes 2097176
  2.2 0.0 copy-start.1
  2.2 0.7 copy-done.1
  2.9 0.0 copy-start.2
  2.9 0.7 copy-done.2
  3.7 0.0 copy-start.3
  3.7 0.7 copy-done.3
  4.4 105.5 %shard_map.109 = (f32[64,64,128]{2,1,0:T(8,128)S(1)}, f32[64,32,128]{2,1,0:T(8,128)S(1)}, f32[32,64]{1,0:T(8,128)S(1)}, f32[32,64]{1,0:T(8,128)S(1)}, f32[32,128]{1,0:T(8,128)S(1)}, /*index=5*/f32[1024,32]{1,0:T(8,128)S(1)}) custom-call(f32[64,64,128]{2,1,0:T(8,128)S(1)} %copy-done, f32[64,64,128]{2,1,0:T(8,128)} %k_ref.1, f32[64,64,128]{2,1,0:T(8,128)} %q_ref.1, ...), custom_call_target="tpu_custom_call" | custom-call | tf_op jit(solution)/shard_map/pallas_call | solution.py:482
  109.9 3.7 %shard_map.110 = (f32[64,64,128]{2,1,0:T(8,128)}, f32[64,64,128]{2,1,0:T(8,128)}, f32[32,64]{1,0:T(8,128)}, f32[32,64]{1,0:T(8,128)}, f32[32,128]{1,0:T(8,128)}, /*index=5*/f32[1024,32]{1,0:T(8,128)}) custom-call(f32[64,64,128]{2,1,0:T(8,128)S(1)} %get-tuple-element.18.t_ref, f32[64,32,128]{2,1,0:T(8,128)S(1)} %get-tuple-element.19.s_ref, ...), custom_call_target="tpu_custom_call" | custom-call | tf_op jit(solution)/shard_map/pallas_call | solution.py:506
Async XLA Ops:
  0.6 1.6 %copy-start = (f32[64,64,128]{2,1,0:T(8,128)S(1)}, f32[64,64,128]{2,1,0:T(8,128)}, u32[]{:S(2)}) copy-start(f32[64,64,128]{2,1,0:T(8,128)} %t0.1) | copy-start | bytes 6291460
  2.2 0.7 copy-start.1
  2.9 0.7 copy-start.2
  3.7 0.7 copy-start.3
